TPU v7x, 128 devices: a whole 4x4x4 slice. The times are simulated.
128 devices in a mesh: dp: 2 (over core), vocab: 64 (over y, z, x).
Axes of the slice: x: 4, y: 4, z: 4, core: 2. Of those that a mesh axis runs over, the one named last changes fastest.
Arguments:
- mentor_score_matrix: bfloat16 [512, 122880], P('dp', 'vocab'), may hold values from -12 to 512
- learner_score_matrix: bfloat16 [512, 262144], P('dp', 'vocab'), may hold values from -12 to 512
- align_dev: int32 [1920, 2], P('vocab'), may hold values from 0 to 63, all different within a row; in each aligned block of 30 rows (0 to 29, 30 to 59, ...) at most 2 rows name the same one
- align_slot: int32 [1920, 2], P('vocab'), may hold values from 0 to 63
- align_weight: bfloat16 [1920, 2, 4096], P('vocab'), may hold values from 0.00077819824 to 0.015625
Outputs:
- scaled_grad: bfloat16 [512, 262144], P('dp', 'vocab')
- divergence_penalty_result: float32 [], replicated
Inputs may be any that keep to these rules, and one draw needn't show every extreme that they name: `align_dev`: the 30 teacher blocks of one vocab shard name each owner at most 2 times in all, and in every draw some shard names some owner exactly 2 times; the 2 owners of one teacher block differ.
All inputs are finite; a program needn't handle non-finite values.
Results may differ from a plain program's by a relative error of at most 0.0039.
Values may be sent and summed in bfloat16 or wider, within the bound.
No kernel may reach another device: no remote copies, remote signals or barrier semaphores. Data moves between devices by JAX's collectives and lax.ppermute only.
A program may use at most 64 MiB of HBM per device.

v0:
```python
import jax
import jax.numpy as jnp
from jax import lax
from jax.sharding import PartitionSpec as P

BLK = 64
SMOOTHING_HEAT = 2


def per_device(mentor_score_matrix, learner_score_matrix, align_dev, align_slot, align_weight):
    smoothing_heat_value = float(SMOOTHING_HEAT)
    owners = lax.axis_size("vocab")
    row_count = mentor_score_matrix.shape[0]
    tb_local = align_dev.shape[0]
    topk = align_dev.shape[1]
    edge_count = tb_local * topk
    most = max(2, 3 * tb_local * topk // (2 * owners))
    sb_local = learner_score_matrix.shape[1] // BLK
    slot_total = owners * most
    mentor_smoothed_scores = mentor_score_matrix.astype(jnp.float32) / smoothing_heat_value
    teacher_local = jnp.max(mentor_smoothed_scores, axis=1)
    teacher_high = lax.pmax(teacher_local, "vocab")
    teacher_exp = jnp.exp(mentor_smoothed_scores - teacher_high[:, None])
    teacher_sum = lax.psum(jnp.sum(teacher_exp, axis=1), "vocab")
    teacher_probs = (teacher_exp / teacher_sum[:, None]).astype(jnp.bfloat16)
    edge_dest = align_dev.reshape(-1)
    dest_hits = (edge_dest[:, None] == jnp.arange(owners, dtype=jnp.int32)[None, :]).astype(
        jnp.int32
    )
    earlier = jnp.sum((jnp.cumsum(dest_hits, axis=0) - dest_hits) * dest_hits, axis=1)
    position = edge_dest * most + earlier
    slot_code = (
        jnp.full((slot_total,), -1.0, jnp.float32)
        .at[position]
        .set(align_slot.reshape(-1).astype(jnp.float32))
        .astype(jnp.bfloat16)
    )
    prob_blocks = teacher_probs.reshape(row_count, tb_local, BLK)
    weight_blocks = align_weight.reshape(tb_local, topk, BLK, BLK)
    edge_terms = (
        jnp.einsum("rbc,bkcd->bkrd", prob_blocks, weight_blocks, preferred_element_type=jnp.float32)
        .astype(jnp.bfloat16)
        .reshape(edge_count, row_count * BLK)
    )
    outgoing = jnp.zeros((slot_total, row_count * BLK), jnp.bfloat16).at[position].set(edge_terms)
    arrived, arrived_code = (
        lax.all_to_all(
            outgoing.reshape(owners, most, row_count * BLK),
            "vocab",
            split_axis=0,
            concat_axis=0,
            tiled=True,
        ),
        lax.all_to_all(
            slot_code.reshape(owners, most), "vocab", split_axis=0, concat_axis=0, tiled=True
        ),
    )
    slot_terms = arrived.reshape(slot_total, row_count, BLK)
    received_code = arrived_code.reshape(-1).astype(jnp.float32)
    learner_smoothed_scores = learner_score_matrix.astype(jnp.float32) / smoothing_heat_value
    student_local = jnp.max(learner_smoothed_scores, axis=1)
    selector = (received_code[:, None] == jnp.arange(sb_local, dtype=jnp.float32)[None, :]).astype(
        jnp.bfloat16
    )
    target = jnp.einsum(
        "ps,prc->rsc", selector, slot_terms, preferred_element_type=jnp.float32
    ).reshape(row_count, sb_local * BLK)
    mass_local = jnp.sum(target, axis=1)
    student_high = lax.pmax(student_local, "vocab")
    student_exp = jnp.exp(learner_smoothed_scores - student_high[:, None])
    student_sum, target_total = lax.psum((jnp.sum(student_exp, axis=1), mass_local), "vocab")
    student_logprob = learner_smoothed_scores - (student_high + jnp.log(student_sum))[:, None]
    vocab_width = float(sb_local * BLK * owners)
    scaled_grad = (
        vocab_width * (target_total[:, None] * jnp.exp(student_logprob) - target)
    ).astype(jnp.bfloat16)
    local_loss = jnp.sum(jax.scipy.special.xlogy(target, target) - target * student_logprob)
    aggregate_divergence = lax.psum(local_loss, ("dp", "vocab"))
    symbol_number_value = float(row_count * lax.axis_size("dp"))
    divergence_penalty_result = (
        smoothing_heat_value * smoothing_heat_value * aggregate_divergence / symbol_number_value
    )
    return (scaled_grad, divergence_penalty_result)


def solution(mesh):
    in_specs = (
        P("dp", "vocab"),
        P("dp", "vocab"),
        P("vocab", None),
        P("vocab", None),
        P("vocab", None, None),
    )
    out_specs = (P("dp", "vocab"), P())
    return jax.shard_map(
        per_device, mesh=mesh, in_specs=in_specs, out_specs=out_specs, check_vma=False
    )
```

profile of v0, /device:TPU:1, one launch (start us, length us, event | category | flops | bytes accessed | tf_op | source)
XLA Modules:
  0.0 729.6 jit_solution(8049112590499290793)
XLA Ops:
  0.6 0.8 copy.23
  1.4 0.7 broadcast_multiply_fusion
  2.1 0.1 eq.28
  2.2 0.1 fusion.12
  2.3 0.1 reduce_window_sum.11
  2.4 0.2 select_reduce_fusion
  2.5 0.1 copy.22
  2.6 0.1 mul.41
  2.8 0.7 convert_element_type.46
  3.4 0.1 copy.27
  3.5 0.1 reshape.91
  3.7 0.8 scatter_custom_fusion.1
  4.4 0.8 all_to_all.12
  5.2 12.0 %all-to-all-start.1 = ((bf16[64,1,2]{2,1,0:T(2,128)(2,1)}), bf16[64,1,2]{2,1,0:T(2,128)(2,1)S(1)}, u32[]{:S(2)}, u32[]{:S(2)}) async-start(bf16[64,1,2]{2,1,0:T(2,128)(2,1)} %all_to_all.12), calls=%async_computation.1 | async-start | bytes 65536 | tf_op jit(solution)/shard_map/all_to_all | solution.py:54
  17.2 3.3 copy.30
  20.5 0.6 fusion.6
  21.0 1.6 copy.24
  22.6 0.3 fusion.10
  22.9 150.7 %all-reduce.1 = (f32[256]{0:T(256)S(1)}, f32[256]{0:T(256)S(1)}) all-reduce(f32[256]{0:T(256)S(1)} %fusion.10, f32[256]{0:T(256)S(1)} %fusion.6), channel_id=1, replica_groups=mesh['dp'=2,'vocab'=64] {'vocab'}, use_global_device_ids=true, to_apply=%region_3.0 | all-reduce | flops 512 | bytes 4096 | tf_op jit(solution)/shard_map/pmax | solution.py:22
  173.6 0.4 fusion.11
  174.1 144.3 %psum.28 = f32[256]{0:T(256)S(1)} all-reduce(f32[256]{0:T(256)S(1)} %fusion.11), channel_id=1, replica_groups=mesh['dp'=2,'vocab'=64] {'vocab'}, use_global_device_ids=true, to_apply=%region_5.6 | all-reduce | flops 256 | bytes 2048 | tf_op jit(solution)/shard_map/psum | solution.py:24
  318.4 1.4 divide_convert_fusion
  319.8 2.9 reshape.73
  322.7 1.6 copy.25
  324.3 1.8 fusion.21
  326.1 1.6 convert_bitcast_fusion
  327.7 4.7 copy.26
  332.3 5.9 reshape.83
  338.3 6.8 scatter_custom_fusion
  345.1 7.6 %reshape.75 = bf16[64,2,16384]{2,1,0:T(2,128)(2,1)} reshape(bf16[128,16384]{1,0:T(8,128)(2,1)} %scatter_custom_fusion) | data formatting | bytes 8388608 | tf_op jit(solution)/shard_map/reshape | solution.py:48
  352.7 0.0 all-to-all-done.1
  352.7 5.7 all-to-all-start
  358.4 0.9 exponential_reduce_fusion
  359.3 0.1 convert_reduce_fusion
  359.4 0.1 reshape.78
  359.6 30.5 %all-to-all-done = bf16[64,2,16384]{2,1,0:T(2,128)(2,1)} async-done(((bf16[64,2,16384]{2,1,0:T(2,128)(2,1)}), bf16[64,2,16384]{2,1,0:T(2,128)(2,1)}, u32[]{:S(2)}, u32[]{:S(2)}) %all-to-all-start) | async-done | bytes 4194336 | tf_op jit(solution)/shard_map/all_to_all | solution.py:47
  390.1 14.6 %reshape.76 = bf16[128,256,64]{2,1,0:T(8,128)(2,1)} reshape(bf16[64,2,16384]{2,1,0:T(2,128)(2,1)} %all-to-all-done) | data formatting | bytes 8388608 | tf_op jit(solution)/shard_map/reshape | solution.py:58
  404.7 10.1 %copy.29 = bf16[128,256,64]{1,0,2:T(8,128)(2,1)} copy(bf16[128,256,64]{2,1,0:T(8,128)(2,1)} %reshape.76) | data formatting | bytes 8388608 | tf_op jit(solution)/shard_map/reshape | solution.py:58
  414.7 5.0 fusion.20
  419.8 149.2 %all-reduce = (f32[256]{0:T(256)S(1)}, f32[256]{0:T(256)S(1)}) all-reduce(f32[256]{0:T(256)S(1)} %exponential_reduce_fusion, f32[256]{0:T(256)S(1)} %get-tuple-element.12), channel_id=1, replica_groups=mesh['dp'=2,'vocab'=64] {'vocab'}, use_global_device_ids=true, to_apply=%region_13.14 | all-reduce | flops 512 | bytes 4096 | tf_op jit(solution)/shard_map/psum | solution.py:71
  569.0 4.6 copy.31
  573.6 4.4 fusion.2
  578.0 4.1 copy.32
  582.1 145.8 %psum.31 = f32[]{:T(128)} all-reduce(f32[]{:T(128)} %get-tuple-element.10), channel_id=1, replica_groups=mesh['dp'=2,'vocab'=64] {'dp','vocab'}, use_global_device_ids=true, to_apply=%region_15.16 | all-reduce | flops 1 | bytes 8 | tf_op jit(solution)/shard_map/psum | solution.py:78
  (3 shorter events, 0.0 us)
Async XLA Ops:
  5.2 347.5 %all-to-all-start.1 = ((bf16[64,1,2]{2,1,0:T(2,128)(2,1)}), bf16[64,1,2]{2,1,0:T(2,128)(2,1)S(1)}, u32[]{:S(2)}, u32[]{:S(2)}) async-start(bf16[64,1,2]{2,1,0:T(2,128)(2,1)} %all_to_all.12), calls=%async_computation.1 | async-start | bytes 65536 | tf_op jit(solution)/shard_map/all_to_all | solution.py:54
  352.7 37.3 %all-to-all-start = ((bf16[64,2,16384]{2,1,0:T(2,128)(2,1)}), bf16[64,2,16384]{2,1,0:T(2,128)(2,1)}, u32[]{:S(2)}, u32[]{:S(2)}) async-start(bf16[64,2,16384]{2,1,0:T(2,128)(2,1)} %reshape.75), calls=%async_computation | async-start | bytes 8388608 | tf_op jit(solution)/shard_map/all_to_all | solution.py:47
where the time goes:
time: 731 us; the launch traced here: 730 us
  blocking collectives  590 us (81%)
  local copies, waits for them, and re-layouts  70.7 us (10%)
  waiting for transfers between devices  30.5 us (4%)
  starting transfers between devices  17.6 us (2%)
  other arithmetic  11.4 us (2%)
    pmax x1, blocking collectives, per_device(): teacher_high = lax.pmax(teacher_local, 'vocab')  151 us
    psum x1, blocking collectives, per_device(): lax.psum((jnp.sum(student_exp, axis=1), mass_local), 'vocab')  149 us
    psum x1, blocking collectives, per_device(): aggregate_divergence = lax.psum(local_loss, ('dp', 'vocab'))  146 us
    psum x1, blocking collectives, per_device(): teacher_sum = lax.psum(jnp.sum(teacher_exp, axis=1), 'vocab')  144 us
    all_to_all x1, waiting for transfers between devices, per_device(): lax.all_to_all(outgoing.reshape(owners, most, row_count * BLK), 'vocab',...  30.5 us
    reshape x2, local copies, waits for them, and re-layouts, per_device(): slot_terms = arrived.reshape(slot_total, row_count, BLK)  24.7 us
  transfers between devices with their start and end apart: 2, of which 1 were waited for; matrix products, arithmetic and copies ran while one was open for 6% of the time, Pallas kernels for 0%

commit v1 on v0

v1 whole, which is shorter than its diff:
```python
import functools

import jax
import jax.numpy as jnp
from jax import lax
from jax.experimental import pallas as pl
from jax.experimental.pallas import tpu as pltpu
from jax.sharding import PartitionSpec as P

BLK = 64
LANES = 128
SMOOTHING_HEAT = 2
MOST = 2
STAT_ROWS = 16
TAIL_ROWS = 24

F32 = jnp.float32
BF16 = jnp.bfloat16


def split2(x):
    hi = x.astype(BF16).astype(F32)
    return hi, x - hi


def send_kernel(dev_ref, slot_ref, x_ref, y_ref, w_ref, out_ref, term, tail, cnt, sem, tail_sem):
    rows, width = x_ref.shape
    owners = out_ref.shape[0]
    halves = rows // LANES
    pairs = width // LANES
    student_tiles = y_ref.shape[1] // LANES
    topk = dev_ref.shape[0]
    block_rows = halves * BLK
    inv_heat = 1.0 / SMOOTHING_HEAT

    high = x_ref[:, :LANES]
    for q in range(1, pairs):
        high = jnp.maximum(high, x_ref[:, q * LANES : (q + 1) * LANES])
    teacher_high = jnp.max(high.astype(F32), axis=1, keepdims=True) * inv_heat

    @pl.loop(0, owners)
    def _(i):
        cnt[i] = 0

    lane = lax.broadcasted_iota(jnp.int32, (BLK, LANES), 1)
    even = lane % 2 == 0
    first = lane < BLK
    code_lane = lax.broadcasted_iota(jnp.int32, (8, LANES), 1)
    code = jnp.full((8, LANES), -1.0, F32)
    high_b = jnp.broadcast_to(teacher_high, (rows, LANES))
    exp_sum = jnp.zeros((rows, LANES), F32)
    mass = jnp.zeros((8, rows), F32)
    copies = []
    for q in range(pairs):
        w = w_ref[q * LANES : (q + 1) * LANES, :].astype(F32).T
        a0, a1 = w[:BLK], w[BLK:]
        l0 = jnp.where(even, a0, pltpu.roll(a1, 1, 1))
        l1 = jnp.where(even, pltpu.roll(a0, LANES - 1, 1), a1)
        lhs = jnp.concatenate(
            [
                jnp.where(first, l0, 0.0),
                jnp.where(first, l1, 0.0),
                jnp.where(first, 0.0, l0),
                jnp.where(first, 0.0, l1),
            ],
            axis=0,
        ).astype(BF16)
        e = jnp.exp(x_ref[:, q * LANES : (q + 1) * LANES].astype(F32) * inv_heat - high_b)
        exp_sum = exp_sum + e
        u = lax.dot_general(
            lhs, e.astype(BF16), (((1,), (1,)), ((), ())), preferred_element_type=F32
        ).astype(BF16)
        mass = mass + jnp.sum(u.astype(F32).reshape(4 * BLK // 8, 8, rows), axis=0)
        for edge in range(2 * topk):
            b, k = 2 * q + edge // topk, edge % topk
            index = q * 2 * topk + edge
            for h in range(halves):
                term[index, h * BLK : (h + 1) * BLK, :] = u[
                    edge * BLK : (edge + 1) * BLK, h * LANES : (h + 1) * LANES
                ]
            dst = dev_ref[k, b]
            at = cnt[dst]
            cnt[dst] = at + 1
            code = jnp.where(code_lane == dst * MOST + at, slot_ref[k, b].astype(F32), code)
            copy = pltpu.make_async_copy(
                term.at[index],
                out_ref.at[dst, pl.ds(pl.multiple_of(at * block_rows, block_rows), block_rows), :],
                sem.at[index],
            )
            copy.start()
            copies.append(copy)

    def student_max(t, m):
        return jnp.maximum(m, y_ref[:, pl.ds(pl.multiple_of(t * LANES, LANES), LANES)])

    m = lax.fori_loop(1, student_tiles, student_max, y_ref[:, :LANES])
    student_high = jnp.max(m.astype(F32), axis=1, keepdims=True) * inv_heat
    student_b = jnp.broadcast_to(student_high, (rows, LANES))

    def student_sum(t, s):
        y = y_ref[:, pl.ds(pl.multiple_of(t * LANES, LANES), LANES)].astype(F32)
        return s + jnp.exp(y * inv_heat - student_b)

    student_exp = lax.fori_loop(0, student_tiles, student_sum, jnp.zeros((rows, LANES), F32))

    row_lane = lax.broadcasted_iota(jnp.int32, (rows, LANES), 1)
    teacher_sum = jnp.sum(exp_sum, axis=1, keepdims=True)
    student_sum_ = jnp.sum(student_exp, axis=1, keepdims=True)
    t_hi, t_lo = split2(teacher_sum)
    s_hi, s_lo = split2(student_sum_)
    columns = jnp.zeros((rows, LANES), F32)
    for i, v in ((0, teacher_high), (1, t_hi), (2, t_lo), (5, student_high), (6, s_hi), (7, s_lo)):
        columns = jnp.where(row_lane == i, v, columns)
    r_hi, r_lo = split2(jnp.sum(mass, axis=0, keepdims=True))
    sub = lax.broadcasted_iota(jnp.int32, (8, LANES), 0)
    pieces = []
    for h in range(halves):
        lanes = slice(h * LANES, (h + 1) * LANES)
        s = columns[lanes].T[:8]
        s = jnp.where(sub == 3, r_hi[:, lanes], s)
        pieces.append(jnp.where(sub == 4, r_lo[:, lanes], s))
    stats = jnp.concatenate(pieces, axis=0).astype(BF16)
    codes = code.astype(BF16)

    @pl.loop(0, owners)
    def _(i):
        tail[i, :STAT_ROWS, :] = stats
        tail[i, STAT_ROWS:, :] = codes

    tail_copy = pltpu.make_async_copy(
        tail, out_ref.at[:, pl.ds(MOST * block_rows, TAIL_ROWS), :], tail_sem
    )
    tail_copy.start()
    for copy in copies:
        copy.wait()
    tail_copy.wait()


def receive_kernel(
    arr_ref, y_ref, out_ref, loss_ref, buf, tail, wide, scale, code_v, code_s, acc, lse_b, mass_b,
    sem, tail_sem, code_sem,
):
    owners = arr_ref.shape[0]
    rows, width = y_ref.shape
    halves = rows // LANES
    tiles = width // LANES
    block_rows = halves * BLK
    groups = sem.shape[0]
    per = owners // groups
    inv_heat = 1.0 / SMOOTHING_HEAT
    vocab_width = float(width * owners)
    me = lax.axis_index("vocab")

    tail_copy = pltpu.make_async_copy(
        arr_ref.at[:, pl.ds(MOST * block_rows, TAIL_ROWS), :], tail, tail_sem
    )
    tail_copy.start()

    def block_copy(g):
        return pltpu.make_async_copy(
            arr_ref.at[pl.ds(g * per, per), pl.ds(0, MOST * block_rows), :],
            buf.at[pl.ds(g * per, per)],
            sem.at[g],
        )

    for g in range(groups):
        block_copy(g).start()

    tail_copy.wait()
    wide[...] = tail[...].astype(F32).reshape(owners * TAIL_ROWS, LANES)
    code_v[...] = wide[pl.ds(STAT_ROWS, owners, stride=TAIL_ROWS), :].astype(jnp.int32)
    code_copy = pltpu.make_async_copy(code_v, code_s, code_sem)
    code_copy.start()

    @pl.loop(0, halves * width // 256)
    def _(i):
        acc[pl.ds(pl.multiple_of(i * 256, 256), 256), :] = jnp.zeros((256, LANES), F32)

    for h in range(halves):
        def stat(i):
            return wide[pl.ds(8 * h + i, owners, stride=TAIL_ROWS), :]

        t_high, s_high = stat(0), stat(5)
        t_top = jnp.max(t_high, axis=0, keepdims=True)
        s_top = jnp.max(s_high, axis=0, keepdims=True)
        t_rel = jnp.exp(t_high - t_top)
        inv = 1.0 / jnp.sum(t_rel * (stat(1) + stat(2)), axis=0, keepdims=True)
        scale_h = t_rel * inv
        scale[h * owners : (h + 1) * owners, :] = scale_h
        total = jnp.sum(scale_h * (stat(3) + stat(4)), axis=0, keepdims=True)
        s_sum = jnp.sum(jnp.exp(s_high - s_top) * (stat(6) + stat(7)), axis=0, keepdims=True)
        lse = s_top + jnp.log(s_sum)
        lse_b[h * LANES : (h + 1) * LANES, :] = jnp.broadcast_to(lse, (LANES, LANES)).T
        mass_b[h * LANES : (h + 1) * LANES, :] = (
            jnp.broadcast_to(total, (LANES, LANES)).T * vocab_width
        )

    code_copy.wait()
    for g in range(groups):
        block_copy(g).wait()

        @pl.loop(0, per)
        def _(i):
            src = g * per + i
            for slot in range(MOST):
                c = code_s[src, me * MOST + slot]

                @pl.when(c >= 0)
                def _():
                    for h in range(halves):
                        at = pl.ds(pl.multiple_of(h * width + c * BLK, BLK), BLK)
                        term = buf[src, slot * block_rows + h * BLK : slot * block_rows + (h + 1) * BLK, :]
                        acc[at, :] = acc[at, :] + term.astype(F32) * scale[pl.ds(h * owners + src, 1), :]

    def tile(t, loss):
        cols = pl.ds(pl.multiple_of(t * LANES, LANES), LANES)
        for h in range(halves):
            lanes = slice(h * LANES, (h + 1) * LANES)
            target = acc[pl.ds(pl.multiple_of(h * width + t * LANES, LANES), LANES), :].T
            logprob = y_ref[lanes, cols].astype(F32) * inv_heat - lse_b[lanes, :]
            out_ref[lanes, cols] = (
                mass_b[lanes, :] * jnp.exp(logprob) - vocab_width * target
            ).astype(BF16)
            loss = loss + jnp.where(target > 0.0, target * (jnp.log(target) - logprob), 0.0)
        return loss

    loss = lax.fori_loop(0, tiles, tile, jnp.zeros((LANES, LANES), F32))
    loss_ref[...] = jnp.broadcast_to(
        jnp.sum(loss, axis=0, keepdims=True).reshape(1, 1, LANES), loss_ref.shape
    )


def per_device(mentor_score_matrix, learner_score_matrix, align_dev, align_slot, align_weight):
    owners = lax.axis_size("vocab")
    shards = owners * lax.axis_size("dp")
    rows, teacher_width = mentor_score_matrix.shape
    width = learner_score_matrix.shape[1]
    tb_local, topk = align_dev.shape
    edges = tb_local * topk
    halves = rows // LANES
    block_rows = halves * BLK
    packet_rows = MOST * block_rows + TAIL_ROWS
    chunks = BLK * BLK // LANES
    weight = (
        align_weight.reshape(tb_local, topk, chunks, LANES)
        .transpose(0, 2, 1, 3)
        .reshape(tb_local * chunks * topk, LANES)
    )
    vmem = pl.BlockSpec(memory_space=pltpu.VMEM)
    smem = pl.BlockSpec(memory_space=pltpu.SMEM)
    hbm = pl.BlockSpec(memory_space=pl.ANY)
    outgoing = pl.pallas_call(
        send_kernel,
        out_shape=jax.ShapeDtypeStruct((owners, packet_rows, LANES), BF16),
        in_specs=[smem, smem, vmem, vmem, vmem],
        out_specs=hbm,
        scratch_shapes=[
            pltpu.VMEM((edges, block_rows, LANES), BF16),
            pltpu.VMEM((owners, TAIL_ROWS, LANES), BF16),
            pltpu.SMEM((owners,), jnp.int32),
            pltpu.SemaphoreType.DMA((edges,)),
            pltpu.SemaphoreType.DMA,
        ],
        name="send",
    )(align_dev.T, align_slot.T, mentor_score_matrix, learner_score_matrix, weight)
    arrived = lax.all_to_all(outgoing, "vocab", split_axis=0, concat_axis=0, tiled=True)
    scaled_grad, loss = pl.pallas_call(
        receive_kernel,
        out_shape=(
            jax.ShapeDtypeStruct((rows, width), BF16),
            jax.ShapeDtypeStruct((shards, 1, LANES), F32),
        ),
        in_specs=[hbm, vmem],
        out_specs=(vmem, vmem),
        scratch_shapes=[
            pltpu.VMEM((owners, MOST * block_rows, LANES), BF16),
            pltpu.VMEM((owners, TAIL_ROWS, LANES), BF16),
            pltpu.VMEM((owners * TAIL_ROWS, LANES), F32),
            pltpu.VMEM((halves * owners, LANES), F32),
            pltpu.VMEM((owners, LANES), jnp.int32),
            pltpu.SMEM((owners, LANES), jnp.int32),
            pltpu.VMEM((halves * width, LANES), F32),
            pltpu.VMEM((rows, LANES), F32),
            pltpu.VMEM((rows, LANES), F32),
            pltpu.SemaphoreType.DMA((8,)),
            pltpu.SemaphoreType.DMA,
            pltpu.SemaphoreType.DMA,
        ],
        name="receive",
    )(arrived, learner_score_matrix)
    parts = lax.all_to_all(loss, ("dp", "vocab"), split_axis=0, concat_axis=0, tiled=True)
    tokens = float(rows * lax.axis_size("dp"))
    divergence = SMOOTHING_HEAT * SMOOTHING_HEAT * jnp.sum(parts) / tokens
    return scaled_grad, divergence


def solution(mesh):
    in_specs = (
        P("dp", "vocab"),
        P("dp", "vocab"),
        P("vocab", None),
        P("vocab", None),
        P("vocab", None, None),
    )
    out_specs = (P("dp", "vocab"), P())
    return jax.shard_map(
        per_device, mesh=mesh, in_specs=in_specs, out_specs=out_specs, check_vma=False
    )
```

time: 731 us -> 108 us (0.15)
  blocking collectives: 590 us -> 83.9 us
  local copies, waits for them, and re-layouts: 70.7 us -> 0 us
  waiting for transfers between devices: 30.5 us -> 0 us
  Pallas kernels: 0 us -> 20.3 us
  starting transfers between devices: 17.6 us -> 0 us
  other arithmetic: 11.4 us -> 0.73 us
    psum x3 -> x0, blocking collectives: 439 us -> none  [the longest x1 149 us: per_device(): lax.psum((jnp.sum(student_exp, axis=1), mass_local), 'vocab')]
    pmax x1 -> x0, blocking collectives: 151 us -> none  [per_device(): teacher_high = lax.pmax(teacher_local, 'vocab')]
    all_to_all x0 -> x2, blocking collectives: none -> 83.9 us  [the longest x1 68 us: per_device(): lax.all_to_all(outgoing, 'vocab', split_axis=0, concat_axis=0, tiled=True)]
    reshape x6 -> x0, local copies, waits for them, and re-layouts: 42.7 us -> none  [the longest x2 24.7 us: per_device(): slot_terms = arrived.reshape(slot_total, row_count, BLK)]
    all_to_all x2 -> x0, waiting for transfers between devices: 30.5 us -> none  [the longest x1 30.5 us: per_device(): lax.all_to_all(outgoing.reshape(owners, most, row_count * BLK), 'vocab',...]
    pallas_call x0 -> x2, Pallas kernels: none -> 20.3 us  [the longest x1 12.1 us: per_device(): pl.pallas_call(receive_kernel, out_shape=(jax.ShapeDtypeStruct((rows, wid...]
    all_to_all x2 -> x0, starting transfers between devices: 17.6 us -> none  [the longest x1 12 us: per_device(): lax.all_to_all(slot_code.reshape(owners, most), 'vocab', split_axis=0, co...]
    unnamed x4 -> x0, local copies, waits for them, and re-layouts: 9.7 us -> none
  transfers between devices with their start and end apart: 2 -> 0, of which waited for: 1 -> 0; matrix products, arithmetic and copies ran while one was open for 6% -> 0% of each run, Pallas kernels for 0% -> 0%
where the time goes in v1:
time: 108 us; the launch traced here: 107 us
  blocking collectives  83.9 us (78%)
  Pallas kernels  20.3 us (19%)
  between operations  2.42 us (2%)
    all_to_all x1, blocking collectives, per_device(): lax.all_to_all(outgoing, 'vocab', split_axis=0, concat_axis=0, tiled=True)  68 us
    all_to_all x1, blocking collectives, per_device(): lax.all_to_all(loss, ('dp', 'vocab'), split_axis=0, concat_axis=0, tiled=...  15.9 us
    pallas_call x1, Pallas kernels, per_device(): pl.pallas_call(receive_kernel, out_shape=(jax.ShapeDtypeStruct((rows, wid...  12.1 us
    pallas_call x1, Pallas kernels, per_device(): pl.pallas_call(send_kernel, out_shape=jax.ShapeDtypeStruct((owners, packe...  8.22 us

profile of v1, /device:TPU:1, one launch (start us, length us, event | category | flops | bytes accessed | tf_op | source)
XLA Modules:
  0.0 107.4 jit_solution(4465060189790334089)
XLA Ops:
  0.6 8.2 %send.1 = bf16[64,280,128]{2,1,0:T(8,128)(2,1)} custom-call(s32[2,30]{1,0:T(2,128)} %bitcast.8, s32[2,30]{1,0:T(2,128)} %bitcast.9, bf16[256,1920]{1,0:T(8,128)(2,1)} %x_ref.1, bf16[256,4096]{1,0:T(8,128)(2,1)} %y_ref.3, bf16[1920,128]{1,0:T(8,128)(2,1)} %bitcast.7), custom_call_target="tpu_custom_call" | custom-call | tf_op jit(solution)/shard_map/send/pallas_call | solution.py:252
  8.9 68.0 %all_to_all.10.arr_ref = bf16[64,280,128]{2,1,0:T(8,128)(2,1)} all-to-all(bf16[64,280,128]{2,1,0:T(8,128)(2,1)} %send.1), channel_id=1, replica_groups=mesh['dp'=2,'vocab'=64] {'vocab'}, dimensions={0} | all-to-all | bytes 9175040 | tf_op jit(solution)/shard_map/all_to_all | solution.py:266
  76.9 12.1 %receive.1 = (bf16[256,4096]{1,0:T(8,128)(2,1)}, f32[128,1,128]{2,1,0:T(1,128)}) custom-call(bf16[64,280,128]{2,1,0:T(8,128)(2,1)} %all_to_all.10.arr_ref, bf16[256,4096]{1,0:T(8,128)(2,1)} %y_ref.3), custom_call_target="tpu_custom_call" | custom-call | tf_op jit(solution)/shard_map/receive/pallas_call | solution.py:267
  89.0 15.9 %all_to_all.11 = f32[128,1,128]{2,1,0:T(1,128)S(1)} all-to-all(f32[128,1,128]{2,1,0:T(1,128)} %get-tuple-element.5), channel_id=1, replica_groups=mesh['dp'=2,'vocab'=64] {'dp','vocab'}, dimensions={0} | all-to-all | bytes 131072 | tf_op jit(solution)/shard_map/all_to_all | solution.py:291
  104.8 0.7 reduce_sum.9

commit v2 on v1

v2 whole, which is shorter than its diff:
```python
import math

import jax
import jax.numpy as jnp
from jax import lax
from jax.experimental import pallas as pl
from jax.experimental.pallas import tpu as pltpu
from jax.sharding import PartitionSpec as P

BLK = 64
LANES = 128
SMOOTHING_HEAT = 2
MOST = 2
STAT_ROWS = 16
TAIL_ROWS = 24
EXP2_SCALE = math.log2(math.e) / SMOOTHING_HEAT
TINY = 2.0**-126

F32 = jnp.float32
BF16 = jnp.bfloat16


def split2(x):
    hi = x.astype(BF16).astype(F32)
    return hi, x - hi


def send_kernel(
    dev_ref, slot_ref, x_ref, y_hbm, w_ref, out_ref, y_ref, probs, term, tail, edge_v, pos_v,
    pos_s, sem, tail_sem, y_sem, pos_sem,
):
    rows, width = x_ref.shape
    owners = out_ref.shape[0]
    halves = rows // LANES
    pairs = width // LANES
    student_tiles = y_ref.shape[1] // LANES
    topk, blocks = dev_ref.shape
    block_rows = halves * BLK
    padded = pos_v.shape[0]

    y_copy = pltpu.make_async_copy(y_hbm, y_ref, y_sem)
    y_copy.start()

    edge_v[...] = jnp.full((8, LANES), -1.0, F32)
    edge_v[:topk, :blocks] = dev_ref[...].astype(F32)
    edge_v[topk : 2 * topk, :blocks] = slot_ref[...].astype(F32)
    edge_rows = edge_v[...]
    edge_cols = edge_rows.T[:padded]
    below = lax.broadcasted_iota(jnp.int32, (padded, LANES), 1) < lax.broadcasted_iota(
        jnp.int32, (padded, LANES), 0
    )
    edge_lane = lax.broadcasted_iota(jnp.int32, (padded, LANES), 1)
    code = jnp.zeros((padded, LANES), F32)
    places = jnp.zeros((padded, LANES), F32)
    for k in range(topk):
        owner = edge_cols[:, k : k + 1]
        hits = jnp.zeros((padded, LANES), F32)
        for other in range(topk):
            same = (owner == edge_rows[other : other + 1, :]) & below
            hits = hits + jnp.where(same, 1.0, 0.0)
        place = owner * MOST + jnp.sum(hits, axis=1, keepdims=True)
        code = code + jnp.where(
            place == edge_lane.astype(F32), edge_cols[:, topk + k : topk + k + 1] + 1.0, 0.0
        )
        places = jnp.where(edge_lane == k, place, places)
    codes = jnp.broadcast_to(jnp.sum(code, axis=0, keepdims=True) - 1.0, (8, LANES)).astype(BF16)
    pos_v[...] = places.astype(jnp.int32)
    pos_copy = pltpu.make_async_copy(pos_v, pos_s, pos_sem)
    pos_copy.start()

    def shard_max(ref, h, tiles):
        lanes = slice(h * LANES, (h + 1) * LANES)
        m = ref[lanes, :LANES]
        for t in range(1, tiles):
            m = jnp.maximum(m, ref[lanes, t * LANES : (t + 1) * LANES])
        return jnp.max(m.astype(F32), axis=1, keepdims=True)

    teacher_high, teacher_sum = [], []
    for h in range(halves):
        lanes = slice(h * LANES, (h + 1) * LANES)
        high = shard_max(x_ref, h, pairs)
        high_b = jnp.broadcast_to(high, (LANES, LANES))
        total = jnp.zeros((LANES, LANES), F32)
        for q in range(pairs):
            e = jnp.exp2((x_ref[lanes, q * LANES : (q + 1) * LANES].astype(F32) - high_b) * EXP2_SCALE)
            total = total + e
            probs[q, lanes, :] = e.astype(BF16)
        teacher_high.append(high)
        teacher_sum.append(jnp.sum(total, axis=1, keepdims=True))

    y_copy.wait()
    student_high = [shard_max(y_ref, h, student_tiles) for h in range(halves)]

    lane = lax.broadcasted_iota(jnp.int32, (BLK, LANES), 1)
    even = lane % 2 == 0
    first = lane < BLK
    mass = jnp.zeros((8, rows), F32)
    for q in range(pairs):
        w = w_ref[q * LANES : (q + 1) * LANES, :].astype(F32).T
        a0, a1 = w[:BLK], w[BLK:]
        l0 = jnp.where(even, a0, pltpu.roll(a1, 1, 1))
        l1 = jnp.where(even, pltpu.roll(a0, LANES - 1, 1), a1)
        lhs = jnp.concatenate(
            [
                jnp.where(first, l0, 0.0),
                jnp.where(first, l1, 0.0),
                jnp.where(first, 0.0, l0),
                jnp.where(first, 0.0, l1),
            ],
            axis=0,
        ).astype(BF16)
        u = lax.dot_general(
            lhs, probs[q], (((1,), (1,)), ((), ())), preferred_element_type=F32
        )
        mass = mass + jnp.sum(u.reshape(4 * BLK // 8, 8, rows), axis=0)
        u = u.astype(BF16)
        for edge in range(2 * topk):
            for h in range(halves):
                term[q * 2 * topk + edge, h * BLK : (h + 1) * BLK, :] = u[
                    edge * BLK : (edge + 1) * BLK, h * LANES : (h + 1) * LANES
                ]

    pos_copy.wait()
    copies = []

    def send_edges(lo, hi):
        for index in range(lo, hi):
            place = pos_s[index // topk, index % topk]
            at = pl.multiple_of((place % MOST) * block_rows, block_rows)
            copy = pltpu.make_async_copy(
                term.at[index], out_ref.at[place // MOST, pl.ds(at, block_rows), :], sem.at[index]
            )
            copy.start()
            copies.append(copy)

    edges = blocks * topk
    steps = halves * student_tiles // 4
    student_sum = []
    for h in range(halves):
        lanes = slice(h * LANES, (h + 1) * LANES)
        high_b = jnp.broadcast_to(student_high[h], (LANES, LANES))
        total = jnp.zeros((LANES, LANES), F32)
        for t in range(student_tiles):
            y = y_ref[lanes, t * LANES : (t + 1) * LANES].astype(F32)
            total = total + jnp.exp2((y - high_b) * EXP2_SCALE)
            if t % 4 == 0:
                step = h * student_tiles // 4 + t // 4
                send_edges(edges * step // steps, edges * (step + 1) // steps)
        student_sum.append(jnp.sum(total, axis=1, keepdims=True))

    row_lane = lax.broadcasted_iota(jnp.int32, (LANES, LANES), 1)
    r_hi, r_lo = split2(jnp.sum(mass, axis=0, keepdims=True))
    sub = lax.broadcasted_iota(jnp.int32, (8, LANES), 0)
    pieces = []
    for h in range(halves):
        t_hi, t_lo = split2(teacher_sum[h])
        s_hi, s_lo = split2(student_sum[h])
        columns = jnp.zeros((LANES, LANES), F32)
        for i, v in (
            (0, teacher_high[h]), (1, t_hi), (2, t_lo), (5, student_high[h]), (6, s_hi), (7, s_lo)
        ):
            columns = jnp.where(row_lane == i, v, columns)
        lanes = slice(h * LANES, (h + 1) * LANES)
        s = columns.T[:8]
        s = jnp.where(sub == 3, r_hi[:, lanes], s)
        pieces.append(jnp.where(sub == 4, r_lo[:, lanes], s))
    stats = jnp.concatenate(pieces, axis=0).astype(BF16)
    for i in range(owners):
        tail[i, :STAT_ROWS, :] = stats
        tail[i, STAT_ROWS:, :] = codes
    tail_copy = pltpu.make_async_copy(
        tail, out_ref.at[:, pl.ds(MOST * block_rows, TAIL_ROWS), :], tail_sem
    )
    tail_copy.start()
    for copy in copies:
        copy.wait()
    tail_copy.wait()


def receive_kernel(
    arr_ref, y_hbm, out_hbm, loss_ref, y_ref, out_ref, buf, tail, wide, scale, code_v, code_s, acc,
    bias, mass_b, sem, tail_sem, code_sem, y_sem, out_sem,
):
    owners = arr_ref.shape[0]
    rows, width = y_ref.shape
    halves = rows // LANES
    tiles = width // LANES
    block_rows = halves * BLK
    groups = sem.shape[0]
    per = owners // groups
    span = width + BLK
    vocab_width = float(width * owners)
    me = lax.axis_index("vocab")

    tail_copy = pltpu.make_async_copy(
        arr_ref.at[:, pl.ds(MOST * block_rows, TAIL_ROWS), :], tail, tail_sem
    )
    tail_copy.start()

    def block_copy(g):
        return pltpu.make_async_copy(
            arr_ref.at[pl.ds(g * per, per), pl.ds(0, MOST * block_rows), :],
            buf.at[pl.ds(g * per, per)],
            sem.at[g],
        )

    for g in range(groups):
        block_copy(g).start()
    y_copy = pltpu.make_async_copy(y_hbm, y_ref, y_sem)
    y_copy.start()

    for h in range(halves):

        @pl.loop(0, width // 512)
        def _(i):
            acc[pl.ds(pl.multiple_of(h * span + i * 512, BLK), 512), :] = jnp.zeros((512, LANES), F32)

    tail_copy.wait()
    wide[...] = tail[...].astype(F32).reshape(owners * TAIL_ROWS, LANES)
    codes = wide[pl.ds(STAT_ROWS, owners, stride=TAIL_ROWS), :].astype(jnp.int32)
    code_v[...] = jnp.where(codes < 0, width // BLK, codes)
    code_copy = pltpu.make_async_copy(code_v, code_s, code_sem)
    code_copy.start()

    for h in range(halves):

        def stat(i):
            return wide[pl.ds(8 * h + i, owners, stride=TAIL_ROWS), :]

        t_high, s_high = stat(0), stat(5)
        t_top = jnp.max(t_high, axis=0, keepdims=True)
        s_top = jnp.max(s_high, axis=0, keepdims=True)
        t_rel = jnp.exp2((t_high - t_top) * EXP2_SCALE)
        s_rel = jnp.exp2((s_high - s_top) * EXP2_SCALE)
        inv = vocab_width / jnp.sum(t_rel * (stat(1) + stat(2)), axis=0, keepdims=True)
        scale_h = t_rel * inv
        scale[h * owners : (h + 1) * owners, :] = scale_h
        total = jnp.sum(scale_h * (stat(3) + stat(4)), axis=0, keepdims=True) * (1.0 / vocab_width)
        s_sum = jnp.sum(s_rel * (stat(6) + stat(7)), axis=0, keepdims=True)
        lse = s_top * EXP2_SCALE + jnp.log2(s_sum) - math.log2(vocab_width)
        bias[h * LANES : (h + 1) * LANES, :] = jnp.broadcast_to(lse, (LANES, LANES)).T
        mass_b[h * LANES : (h + 1) * LANES, :] = jnp.broadcast_to(total, (LANES, LANES)).T

    code_copy.wait()
    for g in range(groups):
        block_copy(g).wait()

        def add_source(i, carry):
            src = g * per + i
            for slot in range(MOST):
                c = code_s[src, me * MOST + slot]
                for h in range(halves):
                    at = pl.ds(pl.multiple_of(h * span + c * BLK, BLK), BLK)
                    lo = slot * block_rows + h * BLK
                    term = buf[src, lo : lo + BLK, :].astype(F32)
                    acc[at, :] = acc[at, :] + term * scale[pl.ds(h * owners + src, 1), :]
            return carry

        lax.fori_loop(0, per, add_source, 0, unroll=2)

    y_copy.wait()
    chunks = out_sem.shape[0]
    chunk = width // chunks

    def tile(t, loss):
        cols = pl.ds(pl.multiple_of(t * LANES, LANES), LANES)
        for h in range(halves):
            lanes = slice(h * LANES, (h + 1) * LANES)
            target = acc[pl.ds(pl.multiple_of(h * span + t * LANES, BLK), LANES), :].T
            logprob = y_ref[lanes, cols].astype(F32) * EXP2_SCALE - bias[lanes, :]
            out_ref[lanes, cols] = (mass_b[lanes, :] * jnp.exp2(logprob) - target).astype(BF16)
            term = target * (jnp.log2(jnp.maximum(target, TINY)) - logprob)
            loss = loss + jnp.sum(term.reshape(LANES // 32, 32, LANES), axis=0)
        return loss

    loss = jnp.zeros((32, LANES), F32)
    out_copies = []
    for i in range(chunks):
        per_chunk = tiles // chunks
        loss = lax.fori_loop(i * per_chunk, (i + 1) * per_chunk, tile, loss, unroll=2)
        part = pl.ds(i * chunk, chunk)
        copy = pltpu.make_async_copy(out_ref.at[:, part], out_hbm.at[:, part], out_sem.at[i])
        copy.start()
        out_copies.append(copy)
    loss_ref[...] = jnp.broadcast_to(
        jnp.sum(loss, axis=0, keepdims=True).reshape(1, 1, LANES), loss_ref.shape
    )
    for copy in out_copies:
        copy.wait()


def per_device(mentor_score_matrix, learner_score_matrix, align_dev, align_slot, align_weight):
    owners = lax.axis_size("vocab")
    shards = owners * lax.axis_size("dp")
    rows, teacher_width = mentor_score_matrix.shape
    width = learner_score_matrix.shape[1]
    tb_local, topk = align_dev.shape
    edges = tb_local * topk
    halves = rows // LANES
    block_rows = halves * BLK
    packet_rows = MOST * block_rows + TAIL_ROWS
    chunks = BLK * BLK // LANES
    weight = (
        align_weight.reshape(tb_local, topk, chunks, LANES)
        .transpose(0, 2, 1, 3)
        .reshape(tb_local * chunks * topk, LANES)
    )
    vmem = pl.BlockSpec(memory_space=pltpu.VMEM)
    hbm = pl.BlockSpec(memory_space=pl.ANY)
    outgoing = pl.pallas_call(
        send_kernel,
        out_shape=jax.ShapeDtypeStruct((owners, packet_rows, LANES), BF16),
        in_specs=[vmem, vmem, vmem, hbm, vmem],
        out_specs=hbm,
        scratch_shapes=[
            pltpu.VMEM((rows, width), BF16),
            pltpu.VMEM((teacher_width // LANES, rows, LANES), BF16),
            pltpu.VMEM((edges, block_rows, LANES), BF16),
            pltpu.VMEM((owners, TAIL_ROWS, LANES), BF16),
            pltpu.VMEM((8, LANES), F32),
            pltpu.VMEM((32, LANES), jnp.int32),
            pltpu.SMEM((32, LANES), jnp.int32),
            pltpu.SemaphoreType.DMA((edges,)),
            pltpu.SemaphoreType.DMA,
            pltpu.SemaphoreType.DMA,
            pltpu.SemaphoreType.DMA,
        ],
        name="send",
    )(align_dev.T, align_slot.T, mentor_score_matrix, learner_score_matrix, weight)
    arrived = lax.all_to_all(outgoing, "vocab", split_axis=0, concat_axis=0, tiled=True)
    scaled_grad, loss = pl.pallas_call(
        receive_kernel,
        out_shape=(
            jax.ShapeDtypeStruct((rows, width), BF16),
            jax.ShapeDtypeStruct((shards, 1, LANES), F32),
        ),
        in_specs=[hbm, hbm],
        out_specs=(hbm, vmem),
        scratch_shapes=[
            pltpu.VMEM((rows, width), BF16),
            pltpu.VMEM((rows, width), BF16),
            pltpu.VMEM((owners, MOST * block_rows, LANES), BF16),
            pltpu.VMEM((owners, TAIL_ROWS, LANES), BF16),
            pltpu.VMEM((owners * TAIL_ROWS, LANES), F32),
            pltpu.VMEM((halves * owners, LANES), F32),
            pltpu.VMEM((owners, LANES), jnp.int32),
            pltpu.SMEM((owners, LANES), jnp.int32),
            pltpu.VMEM((halves * (width + BLK), LANES), F32),
            pltpu.VMEM((rows, LANES), F32),
            pltpu.VMEM((rows, LANES), F32),
            pltpu.SemaphoreType.DMA((8,)),
            pltpu.SemaphoreType.DMA,
            pltpu.SemaphoreType.DMA,
            pltpu.SemaphoreType.DMA,
            pltpu.SemaphoreType.DMA((8,)),
        ],
        name="receive",
    )(arrived, learner_score_matrix)
    parts = lax.all_to_all(loss, ("dp", "vocab"), split_axis=0, concat_axis=0, tiled=True)
    tokens = float(rows * lax.axis_size("dp"))
    unit = math.log(2.0) / (width * owners)
    divergence = SMOOTHING_HEAT * SMOOTHING_HEAT * unit / tokens * jnp.sum(parts)
    return scaled_grad, divergence


def solution(mesh):
    in_specs = (
        P("dp", "vocab"),
        P("dp", "vocab"),
        P("vocab", None),
        P("vocab", None),
        P("vocab", None, None),
    )
    out_specs = (P("dp", "vocab"), P())
    return jax.shard_map(
        per_device, mesh=mesh, in_specs=in_specs, out_specs=out_specs, check_vma=False
    )
```

time: 108 us -> 102 us (0.944)
  Pallas kernels: 20.3 us -> 14.7 us
    pallas_call x1, Pallas kernels: 12.1 us -> 8.38 us  [per_device(): pl.pallas_call(receive_kernel, out_shape=(jax.ShapeDtypeStruct((rows, wid...]
    pallas_call x1, Pallas kernels: 8.22 us -> 6.31 us  [per_device(): pl.pallas_call(send_kernel, out_shape=jax.ShapeDtypeStruct((owners, packe...]
where the time goes in v2:
time: 102 us
  blocking collectives  83.9 us (82%)
  Pallas kernels  14.7 us (14%)
  between operations  2.42 us (2%)
    all_to_all x1, blocking collectives, per_device(): lax.all_to_all(outgoing, 'vocab', split_axis=0, concat_axis=0, tiled=True)  68.1 us
    all_to_all x1, blocking collectives, per_device(): lax.all_to_all(loss, ('dp', 'vocab'), split_axis=0, concat_axis=0, tiled=...  15.8 us
    pallas_call x1, Pallas kernels, per_device(): pl.pallas_call(receive_kernel, out_shape=(jax.ShapeDtypeStruct((rows, wid...  8.38 us
    pallas_call x1, Pallas kernels, per_device(): pl.pallas_call(send_kernel, out_shape=jax.ShapeDtypeStruct((owners, packe...  6.31 us

profile of v2, /device:TPU:1, one launch (start us, length us, event | category | flops | bytes accessed | tf_op | source)
XLA Modules:
  0.0 101.7 jit_solution(18025592159239496559)
XLA Ops:
  0.6 6.3 %send.1 = bf16[64,280,128]{2,1,0:T(8,128)(2,1)} custom-call(s32[2,30]{1,0:T(2,128)} %bitcast.8, s32[2,30]{1,0:T(2,128)} %bitcast.9, bf16[256,1920]{1,0:T(8,128)(2,1)} %x_ref.1, bf16[256,4096]{1,0:T(8,128)(2,1)} %y_hbm.3, bf16[1920,128]{1,0:T(8,128)(2,1)} %bitcast.7), custom_call_target="tpu_custom_call" | custom-call | tf_op jit(solution)/shard_map/send/pallas_call | solution.py:310
  7.0 68.1 %all_to_all.10.arr_ref = bf16[64,280,128]{2,1,0:T(8,128)(2,1)} all-to-all(bf16[64,280,128]{2,1,0:T(8,128)(2,1)} %send.1), channel_id=1, replica_groups=mesh['dp'=2,'vocab'=64] {'vocab'}, dimensions={0} | all-to-all | bytes 9175040 | tf_op jit(solution)/shard_map/all_to_all | solution.py:330
  75.0 8.4 %receive.1 = (bf16[256,4096]{1,0:T(8,128)(2,1)}, f32[128,1,128]{2,1,0:T(1,128)}) custom-call(bf16[64,280,128]{2,1,0:T(8,128)(2,1)} %all_to_all.10.arr_ref, bf16[256,4096]{1,0:T(8,128)(2,1)} %y_hbm.3), custom_call_target="tpu_custom_call" | custom-call | tf_op jit(solution)/shard_map/receive/pallas_call | solution.py:331
  83.4 15.8 %all_to_all.11 = f32[128,1,128]{2,1,0:T(1,128)S(1)} all-to-all(f32[128,1,128]{2,1,0:T(1,128)} %get-tuple-element.5), channel_id=1, replica_groups=mesh['dp'=2,'vocab'=64] {'dp','vocab'}, dimensions={0} | all-to-all | bytes 131072 | tf_op jit(solution)/shard_map/all_to_all | solution.py:359
  99.2 0.7 reduce_sum.9

commit v3 on v2

--- a/solution.py
+++ b/solution.py
@@ -11,8 +11,8 @@
 LANES = 128
 SMOOTHING_HEAT = 2
 MOST = 2
-STAT_ROWS = 16
-TAIL_ROWS = 24
+TAIL_ROWS = 16
+CODE_ROW = 7
 EXP2_SCALE = math.log2(math.e) / SMOOTHING_HEAT
 TINY = 2.0**-126
 
@@ -26,7 +26,7 @@
 
 
 def send_kernel(
-    dev_ref, slot_ref, x_ref, y_hbm, w_ref, out_ref, y_ref, probs, term, tail, edge_v, pos_v,
+    dev_ref, slot_ref, x_ref, y_hbm, w_ref, out_ref, y_ref, probs, high_v, term, tail, edge_v, pos_v,
     pos_s, sem, tail_sem, y_sem, pos_sem,
 ):
     rows, width = x_ref.shape
@@ -63,7 +63,7 @@
             place == edge_lane.astype(F32), edge_cols[:, topk + k : topk + k + 1] + 1.0, 0.0
         )
         places = jnp.where(edge_lane == k, place, places)
-    codes = jnp.broadcast_to(jnp.sum(code, axis=0, keepdims=True) - 1.0, (8, LANES)).astype(BF16)
+    codes = jnp.sum(code, axis=0, keepdims=True) - 1.0
     pos_v[...] = places.astype(jnp.int32)
     pos_copy = pltpu.make_async_copy(pos_v, pos_s, pos_sem)
     pos_copy.start()
@@ -91,10 +91,24 @@
     y_copy.wait()
     student_high = [shard_max(y_ref, h, student_tiles) for h in range(halves)]
 
+    pos_copy.wait()
+
+    def send_edges(q):
+        for index in range(q * 2 * topk, (q + 1) * 2 * topk):
+            place = pos_s[index // topk, index % topk]
+            at = pl.multiple_of((place % MOST) * block_rows, block_rows)
+            pltpu.make_async_copy(
+                term.at[index], out_ref.at[place // MOST, pl.ds(at, block_rows), :], sem
+            ).start()
+
+    for h in range(halves):
+        high_v[h] = jnp.broadcast_to(student_high[h], (LANES, LANES))
     lane = lax.broadcasted_iota(jnp.int32, (BLK, LANES), 1)
     even = lane % 2 == 0
     first = lane < BLK
     mass = jnp.zeros((8, rows), F32)
+    student_total = [jnp.zeros((LANES, LANES), F32) for _ in range(halves)]
+    items = [(h, t) for h in range(halves) for t in range(student_tiles)]
     for q in range(pairs):
         w = w_ref[q * LANES : (q + 1) * LANES, :].astype(F32).T
         a0, a1 = w[:BLK], w[BLK:]
@@ -112,6 +126,9 @@
         u = lax.dot_general(
             lhs, probs[q], (((1,), (1,)), ((), ())), preferred_element_type=F32
         )
+        for h, t in items[len(items) * q // pairs : len(items) * (q + 1) // pairs]:
+            y = y_ref[h * LANES : (h + 1) * LANES, t * LANES : (t + 1) * LANES].astype(F32)
+            student_total[h] = student_total[h] + jnp.exp2((y - high_v[h]) * EXP2_SCALE)
         mass = mass + jnp.sum(u.reshape(4 * BLK // 8, 8, rows), axis=0)
         u = u.astype(BF16)
         for edge in range(2 * topk):
@@ -119,34 +136,9 @@
                 term[q * 2 * topk + edge, h * BLK : (h + 1) * BLK, :] = u[
                     edge * BLK : (edge + 1) * BLK, h * LANES : (h + 1) * LANES
                 ]
-
-    pos_copy.wait()
-    copies = []
-
-    def send_edges(lo, hi):
-        for index in range(lo, hi):
-            place = pos_s[index // topk, index % topk]
-            at = pl.multiple_of((place % MOST) * block_rows, block_rows)
-            copy = pltpu.make_async_copy(
-                term.at[index], out_ref.at[place // MOST, pl.ds(at, block_rows), :], sem.at[index]
-            )
-            copy.start()
-            copies.append(copy)
-
-    edges = blocks * topk
-    steps = halves * student_tiles // 4
-    student_sum = []
-    for h in range(halves):
-        lanes = slice(h * LANES, (h + 1) * LANES)
-        high_b = jnp.broadcast_to(student_high[h], (LANES, LANES))
-        total = jnp.zeros((LANES, LANES), F32)
-        for t in range(student_tiles):
-            y = y_ref[lanes, t * LANES : (t + 1) * LANES].astype(F32)
-            total = total + jnp.exp2((y - high_b) * EXP2_SCALE)
-            if t % 4 == 0:
-                step = h * student_tiles // 4 + t // 4
-                send_edges(edges * step // steps, edges * (step + 1) // steps)
-        student_sum.append(jnp.sum(total, axis=1, keepdims=True))
+        if q > 0:
+            send_edges(q - 1)
+    send_edges(pairs - 1)
 
     row_lane = lax.broadcasted_iota(jnp.int32, (LANES, LANES), 1)
     r_hi, r_lo = split2(jnp.sum(mass, axis=0, keepdims=True))
@@ -154,32 +146,30 @@
     pieces = []
     for h in range(halves):
         t_hi, t_lo = split2(teacher_sum[h])
-        s_hi, s_lo = split2(student_sum[h])
+        student_sum = jnp.sum(student_total[h], axis=1, keepdims=True)
+        s_hi, s_lo = split2(student_high[h] * EXP2_SCALE + jnp.log2(student_sum))
         columns = jnp.zeros((LANES, LANES), F32)
-        for i, v in (
-            (0, teacher_high[h]), (1, t_hi), (2, t_lo), (5, student_high[h]), (6, s_hi), (7, s_lo)
-        ):
+        for i, v in ((0, teacher_high[h]), (1, t_hi), (2, t_lo), (5, s_hi), (6, s_lo)):
             columns = jnp.where(row_lane == i, v, columns)
         lanes = slice(h * LANES, (h + 1) * LANES)
         s = columns.T[:8]
         s = jnp.where(sub == 3, r_hi[:, lanes], s)
-        pieces.append(jnp.where(sub == 4, r_lo[:, lanes], s))
+        s = jnp.where(sub == 4, r_lo[:, lanes], s)
+        pieces.append(jnp.where(sub == CODE_ROW, codes, s))
     stats = jnp.concatenate(pieces, axis=0).astype(BF16)
     for i in range(owners):
-        tail[i, :STAT_ROWS, :] = stats
-        tail[i, STAT_ROWS:, :] = codes
+        tail[i] = stats
     tail_copy = pltpu.make_async_copy(
         tail, out_ref.at[:, pl.ds(MOST * block_rows, TAIL_ROWS), :], tail_sem
     )
     tail_copy.start()
-    for copy in copies:
-        copy.wait()
+    pltpu.make_async_copy(term, term, sem).wait()
     tail_copy.wait()
 
 
 def receive_kernel(
     arr_ref, y_hbm, out_hbm, loss_ref, y_ref, out_ref, buf, tail, wide, scale, code_v, code_s, acc,
-    bias, mass_b, sem, tail_sem, code_sem, y_sem, out_sem,
+    bias, sem, tail_sem, code_sem, y_sem, out_sem,
 ):
     owners = arr_ref.shape[0]
     rows, width = y_ref.shape
@@ -213,33 +203,34 @@
 
         @pl.loop(0, width // 512)
         def _(i):
-            acc[pl.ds(pl.multiple_of(h * span + i * 512, BLK), 512), :] = jnp.zeros((512, LANES), F32)
+            acc[pl.ds(pl.multiple_of(h * span + i * 512, BLK), 512), :] = jnp.full((512, LANES), TINY, F32)
 
     tail_copy.wait()
     wide[...] = tail[...].astype(F32).reshape(owners * TAIL_ROWS, LANES)
-    codes = wide[pl.ds(STAT_ROWS, owners, stride=TAIL_ROWS), :].astype(jnp.int32)
+    codes = wide[pl.ds(CODE_ROW, owners, stride=TAIL_ROWS), :].astype(jnp.int32)
     code_v[...] = jnp.where(codes < 0, width // BLK, codes)
     code_copy = pltpu.make_async_copy(code_v, code_s, code_sem)
     code_copy.start()
 
+    row_terms = jnp.zeros((1, LANES), F32)
     for h in range(halves):
 
         def stat(i):
             return wide[pl.ds(8 * h + i, owners, stride=TAIL_ROWS), :]
 
-        t_high, s_high = stat(0), stat(5)
+        t_high = stat(0)
         t_top = jnp.max(t_high, axis=0, keepdims=True)
-        s_top = jnp.max(s_high, axis=0, keepdims=True)
         t_rel = jnp.exp2((t_high - t_top) * EXP2_SCALE)
-        s_rel = jnp.exp2((s_high - s_top) * EXP2_SCALE)
         inv = vocab_width / jnp.sum(t_rel * (stat(1) + stat(2)), axis=0, keepdims=True)
         scale_h = t_rel * inv
         scale[h * owners : (h + 1) * owners, :] = scale_h
-        total = jnp.sum(scale_h * (stat(3) + stat(4)), axis=0, keepdims=True) * (1.0 / vocab_width)
-        s_sum = jnp.sum(s_rel * (stat(6) + stat(7)), axis=0, keepdims=True)
-        lse = s_top * EXP2_SCALE + jnp.log2(s_sum) - math.log2(vocab_width)
-        bias[h * LANES : (h + 1) * LANES, :] = jnp.broadcast_to(lse, (LANES, LANES)).T
-        mass_b[h * LANES : (h + 1) * LANES, :] = jnp.broadcast_to(total, (LANES, LANES)).T
+        total = jnp.sum(scale_h * (stat(3) + stat(4)), axis=0, keepdims=True)
+        log_total = jnp.log2(total)
+        s_lse = stat(5) + stat(6)
+        s_top = jnp.max(s_lse, axis=0, keepdims=True)
+        lse = s_top + jnp.log2(jnp.sum(jnp.exp2(s_lse - s_top), axis=0, keepdims=True))
+        bias[h * LANES : (h + 1) * LANES, :] = jnp.broadcast_to(lse - log_total, (LANES, LANES)).T
+        row_terms = row_terms + total * (log_total - math.log2(vocab_width)) * (1.0 / owners)
 
     code_copy.wait()
     for g in range(groups):
@@ -267,9 +258,9 @@
         for h in range(halves):
             lanes = slice(h * LANES, (h + 1) * LANES)
             target = acc[pl.ds(pl.multiple_of(h * span + t * LANES, BLK), LANES), :].T
-            logprob = y_ref[lanes, cols].astype(F32) * EXP2_SCALE - bias[lanes, :]
-            out_ref[lanes, cols] = (mass_b[lanes, :] * jnp.exp2(logprob) - target).astype(BF16)
-            term = target * (jnp.log2(jnp.maximum(target, TINY)) - logprob)
+            goal = y_ref[lanes, cols].astype(F32) * EXP2_SCALE - bias[lanes, :]
+            out_ref[lanes, cols] = (jnp.exp2(goal) - target).astype(BF16)
+            term = target * (jnp.log2(target) - goal)
             loss = loss + jnp.sum(term.reshape(LANES // 32, 32, LANES), axis=0)
         return loss
 
@@ -283,7 +274,7 @@
         copy.start()
         out_copies.append(copy)
     loss_ref[...] = jnp.broadcast_to(
-        jnp.sum(loss, axis=0, keepdims=True).reshape(1, 1, LANES), loss_ref.shape
+        (jnp.sum(loss, axis=0, keepdims=True) + row_terms).reshape(1, 1, LANES), loss_ref.shape
     )
     for copy in out_copies:
         copy.wait()
@@ -315,12 +306,13 @@
         scratch_shapes=[
             pltpu.VMEM((rows, width), BF16),
             pltpu.VMEM((teacher_width // LANES, rows, LANES), BF16),
+            pltpu.VMEM((halves, LANES, LANES), F32),
             pltpu.VMEM((edges, block_rows, LANES), BF16),
             pltpu.VMEM((owners, TAIL_ROWS, LANES), BF16),
             pltpu.VMEM((8, LANES), F32),
             pltpu.VMEM((32, LANES), jnp.int32),
             pltpu.SMEM((32, LANES), jnp.int32),
-            pltpu.SemaphoreType.DMA((edges,)),
+            pltpu.SemaphoreType.DMA,
             pltpu.SemaphoreType.DMA,
             pltpu.SemaphoreType.DMA,
             pltpu.SemaphoreType.DMA,
@@ -347,7 +339,6 @@
             pltpu.SMEM((owners, LANES), jnp.int32),
             pltpu.VMEM((halves * (width + BLK), LANES), F32),
             pltpu.VMEM((rows, LANES), F32),
-            pltpu.VMEM((rows, LANES), F32),
             pltpu.SemaphoreType.DMA((8,)),
             pltpu.SemaphoreType.DMA,
             pltpu.SemaphoreType.DMA,

time: 102 us -> 100 us (0.980)
  blocking collectives: 83.9 us -> 82.5 us
    all_to_all x1, blocking collectives: 68.1 us -> 66.6 us  [per_device(): lax.all_to_all(outgoing, 'vocab', split_axis=0, concat_axis=0, tiled=True)]
where the time goes in v3:
time: 100 us; the launch traced here: 99.7 us
  blocking collectives  82.5 us (82%)
  Pallas kernels  14.1 us (14%)
  between operations  2.42 us (2%)
    all_to_all x1, blocking collectives, per_device(): lax.all_to_all(outgoing, 'vocab', split_axis=0, concat_axis=0, tiled=True)  66.6 us
    all_to_all x1, blocking collectives, per_device(): lax.all_to_all(loss, ('dp', 'vocab'), split_axis=0, concat_axis=0, tiled=...  15.9 us
    pallas_call x1, Pallas kernels, per_device(): pl.pallas_call(receive_kernel, out_shape=(jax.ShapeDtypeStruct((rows, wid...  8.35 us
    pallas_call x1, Pallas kernels, per_device(): pl.pallas_call(send_kernel, out_shape=jax.ShapeDtypeStruct((owners, packe...  5.74 us

profile of v3, /device:TPU:1, one launch (start us, length us, event | category | flops | bytes accessed | tf_op | source)
XLA Modules:
  0.0 99.7 jit_solution(18337752288817314143)
XLA Ops:
  0.6 5.7 %send.1 = bf16[64,272,128]{2,1,0:T(8,128)(2,1)} custom-call(s32[2,30]{1,0:T(2,128)} %bitcast.8, s32[2,30]{1,0:T(2,128)} %bitcast.9, bf16[256,1920]{1,0:T(8,128)(2,1)} %x_ref.1, bf16[256,4096]{1,0:T(8,128)(2,1)} %y_hbm.3, bf16[1920,128]{1,0:T(8,128)(2,1)} %bitcast.7), custom_call_target="tpu_custom_call" | custom-call | tf_op jit(solution)/shard_map/send/pallas_call | solution.py:301
  6.4 66.6 %all_to_all.10.arr_ref = bf16[64,272,128]{2,1,0:T(8,128)(2,1)} all-to-all(bf16[64,272,128]{2,1,0:T(8,128)(2,1)} %send.1), channel_id=1, replica_groups=mesh['dp'=2,'vocab'=64] {'vocab'}, dimensions={0} | all-to-all | bytes 8912896 | tf_op jit(solution)/shard_map/all_to_all | solution.py:322
  73.0 8.3 %receive.1 = (bf16[256,4096]{1,0:T(8,128)(2,1)}, f32[128,1,128]{2,1,0:T(1,128)}) custom-call(bf16[64,272,128]{2,1,0:T(8,128)(2,1)} %all_to_all.10.arr_ref, bf16[256,4096]{1,0:T(8,128)(2,1)} %y_hbm.3), custom_call_target="tpu_custom_call" | custom-call | tf_op jit(solution)/shard_map/receive/pallas_call | solution.py:323
  81.3 15.9 %all_to_all.11 = f32[128,1,128]{2,1,0:T(1,128)S(1)} all-to-all(f32[128,1,128]{2,1,0:T(1,128)} %get-tuple-element.5), channel_id=1, replica_groups=mesh['dp'=2,'vocab'=64] {'dp','vocab'}, dimensions={0} | all-to-all | bytes 131072 | tf_op jit(solution)/shard_map/all_to_all | solution.py:350
  97.2 0.7 reduce_sum.9

commit v4 on v3

--- a/solution.py
+++ b/solution.py
@@ -172,7 +172,7 @@
     bias, sem, tail_sem, code_sem, y_sem, out_sem,
 ):
     owners = arr_ref.shape[0]
-    rows, width = y_ref.shape
+    width, rows = y_ref.shape
     halves = rows // LANES
     tiles = width // LANES
     block_rows = halves * BLK
@@ -229,7 +229,7 @@
         s_lse = stat(5) + stat(6)
         s_top = jnp.max(s_lse, axis=0, keepdims=True)
         lse = s_top + jnp.log2(jnp.sum(jnp.exp2(s_lse - s_top), axis=0, keepdims=True))
-        bias[h * LANES : (h + 1) * LANES, :] = jnp.broadcast_to(lse - log_total, (LANES, LANES)).T
+        bias[h : h + 1, :] = lse - log_total
         row_terms = row_terms + total * (log_total - math.log2(vocab_width)) * (1.0 / owners)
 
     code_copy.wait()
@@ -257,9 +257,9 @@
         cols = pl.ds(pl.multiple_of(t * LANES, LANES), LANES)
         for h in range(halves):
             lanes = slice(h * LANES, (h + 1) * LANES)
-            target = acc[pl.ds(pl.multiple_of(h * span + t * LANES, BLK), LANES), :].T
-            goal = y_ref[lanes, cols].astype(F32) * EXP2_SCALE - bias[lanes, :]
-            out_ref[lanes, cols] = (jnp.exp2(goal) - target).astype(BF16)
+            target = acc[pl.ds(pl.multiple_of(h * span + t * LANES, BLK), LANES), :]
+            goal = y_ref[cols, lanes].astype(F32) * EXP2_SCALE - bias[h : h + 1, :]
+            out_ref[lanes, cols] = (jnp.exp2(goal) - target).astype(BF16).T
             term = target * (jnp.log2(target) - goal)
             loss = loss + jnp.sum(term.reshape(LANES // 32, 32, LANES), axis=0)
         return loss
@@ -268,7 +268,7 @@
     out_copies = []
     for i in range(chunks):
         per_chunk = tiles // chunks
-        loss = lax.fori_loop(i * per_chunk, (i + 1) * per_chunk, tile, loss, unroll=2)
+        loss = lax.fori_loop(i * per_chunk, (i + 1) * per_chunk, tile, loss, unroll=True)
         part = pl.ds(i * chunk, chunk)
         copy = pltpu.make_async_copy(out_ref.at[:, part], out_hbm.at[:, part], out_sem.at[i])
         copy.start()
@@ -329,7 +329,7 @@
         in_specs=[hbm, hbm],
         out_specs=(hbm, vmem),
         scratch_shapes=[
-            pltpu.VMEM((rows, width), BF16),
+            pltpu.VMEM((width, rows), BF16),
             pltpu.VMEM((rows, width), BF16),
             pltpu.VMEM((owners, MOST * block_rows, LANES), BF16),
             pltpu.VMEM((owners, TAIL_ROWS, LANES), BF16),
@@ -338,7 +338,7 @@
             pltpu.VMEM((owners, LANES), jnp.int32),
             pltpu.SMEM((owners, LANES), jnp.int32),
             pltpu.VMEM((halves * (width + BLK), LANES), F32),
-            pltpu.VMEM((rows, LANES), F32),
+            pltpu.VMEM((8, LANES), F32),
             pltpu.SemaphoreType.DMA((8,)),
             pltpu.SemaphoreType.DMA,
             pltpu.SemaphoreType.DMA,
@@ -346,7 +346,7 @@
             pltpu.SemaphoreType.DMA((8,)),
         ],
         name="receive",
-    )(arrived, learner_score_matrix)
+    )(arrived, learner_score_matrix.T)
     parts = lax.all_to_all(loss, ("dp", "vocab"), split_axis=0, concat_axis=0, tiled=True)
     tokens = float(rows * lax.axis_size("dp"))
     unit = math.log(2.0) / (width * owners)

time: 100 us -> 101 us (1.010)
  blocking collectives: 82.5 us -> 15.7 us
  waiting for transfers between devices: 0 us -> 54.2 us
  starting transfers between devices: 0 us -> 12.3 us
  local copies, waits for them, and re-layouts: 0 us -> 2.58 us
  Pallas kernels: 14.1 us -> 12.9 us
    all_to_all x1 -> x0, blocking collectives: 66.6 us -> none  [per_device(): lax.all_to_all(outgoing, 'vocab', split_axis=0, concat_axis=0, tiled=True)]
    all_to_all x0 -> x1, waiting for transfers between devices: none -> 54.2 us  [per_device(): lax.all_to_all(outgoing, 'vocab', split_axis=0, concat_axis=0, tiled=True)]
    all_to_all x0 -> x1, starting transfers between devices: none -> 12.3 us  [per_device(): lax.all_to_all(outgoing, 'vocab', split_axis=0, concat_axis=0, tiled=True)]
    unnamed x0 -> x3, local copies, waits for them, and re-layouts: none -> 2.58 us
    pallas_call x1, Pallas kernels: 8.35 us -> 7.23 us  [per_device(): pl.pallas_call(receive_kernel, out_shape=(jax.ShapeDtypeStruct((rows, wid...]
  transfers between devices with their start and end apart: 0 -> 1, of which waited for: 0 -> 1; matrix products, arithmetic and copies ran while one was open for 0% -> 3% of each run, Pallas kernels for 0% -> 0%
where the time goes in v4:
time: 101 us
  waiting for transfers between devices  54.2 us (54%)
  blocking collectives  15.7 us (16%)
  Pallas kernels  12.9 us (13%)
  starting transfers between devices  12.3 us (12%)
  local copies, waits for them, and re-layouts  2.58 us (3%)
  between operations  2.45 us (2%)
    all_to_all x1, waiting for transfers between devices, per_device(): lax.all_to_all(outgoing, 'vocab', split_axis=0, concat_axis=0, tiled=True)  54.2 us
    all_to_all x1, blocking collectives, per_device(): lax.all_to_all(loss, ('dp', 'vocab'), split_axis=0, concat_axis=0, tiled=...  15.7 us
    all_to_all x1, starting transfers between devices, per_device(): lax.all_to_all(outgoing, 'vocab', split_axis=0, concat_axis=0, tiled=True)  12.3 us
    pallas_call x1, Pallas kernels, per_device(): pl.pallas_call(receive_kernel, out_shape=(jax.ShapeDtypeStruct((rows, wid...  7.23 us
    pallas_call x1, Pallas kernels, per_device(): pl.pallas_call(send_kernel, out_shape=jax.ShapeDtypeStruct((owners, packe...  5.71 us
    unnamed x3, local copies, waits for them, and re-layouts  2.58 us
  transfers between devices with their start and end apart: 1, of which 1 were waited for; matrix products, arithmetic and copies ran while one was open for 3% of the time, Pallas kernels for 0%

profile of v4, /device:TPU:1, one launch (start us, length us, event | category | flops | bytes accessed | tf_op | source)
XLA Modules:
  0.0 100.9 jit_solution(5135068675183917593)
XLA Ops:
  0.6 5.7 %send.1 = bf16[64,272,128]{2,1,0:T(8,128)(2,1)} custom-call(s32[2,30]{1,0:T(2,128)} %bitcast.10, s32[2,30]{1,0:T(2,128)} %bitcast.11, bf16[256,1920]{1,0:T(8,128)(2,1)} %x_ref.1, bf16[256,4096]{1,0:T(8,128)(2,1)} %y_hbm.1, bf16[1920,128]{1,0:T(8,128)(2,1)} %bitcast.9), custom_call_target="tpu_custom_call" | custom-call | tf_op jit(solution)/shard_map/send/pallas_call | solution.py:301
  6.4 0.0 copy-start
  6.4 12.3 %all-to-all-start = ((bf16[64,272,128]{2,1,0:T(8,128)(2,1)}), bf16[64,272,128]{2,1,0:T(8,128)(2,1)}, u32[]{:S(2)}, u32[]{:S(2)}) async-start(bf16[64,272,128]{2,1,0:T(8,128)(2,1)} %send.1), calls=%async_computation | async-start | bytes 8912896 | tf_op jit(solution)/shard_map/all_to_all | solution.py:322
  18.7 0.0 copy-done
  18.7 2.6 %copy.8 = bf16[256,4096]{0,1:T(8,128)(2,1)} copy(bf16[256,4096]{1,0:T(8,128)(2,1)S(1)} %copy-done) | data formatting | bytes 4194304 | tf_op args[1]
  21.3 54.2 %all-to-all-done.arr_ref = bf16[64,272,128]{2,1,0:T(8,128)(2,1)} async-done(((bf16[64,272,128]{2,1,0:T(8,128)(2,1)}), bf16[64,272,128]{2,1,0:T(8,128)(2,1)}, u32[]{:S(2)}, u32[]{:S(2)}) %all-to-all-start) | async-done | bytes 4456480 | tf_op jit(solution)/shard_map/all_to_all | solution.py:322
  75.5 7.2 %receive.1 = (bf16[256,4096]{1,0:T(8,128)(2,1)}, f32[128,1,128]{2,1,0:T(1,128)}) custom-call(bf16[64,272,128]{2,1,0:T(8,128)(2,1)} %all-to-all-done.arr_ref, bf16[4096,256]{1,0:T(8,128)(2,1)} %bitcast.8), custom_call_target="tpu_custom_call" | custom-call | tf_op jit(solution)/shard_map/receive/pallas_call | solution.py:323
  82.7 15.7 %all_to_all.10 = f32[128,1,128]{2,1,0:T(1,128)S(1)} all-to-all(f32[128,1,128]{2,1,0:T(1,128)} %get-tuple-element.5), channel_id=1, replica_groups=mesh['dp'=2,'vocab'=64] {'dp','vocab'}, dimensions={0} | all-to-all | bytes 131072 | tf_op jit(solution)/shard_map/all_to_all | solution.py:350
  98.4 0.7 reduce_sum.9
Async XLA Ops:
  6.4 12.4 %copy-start = (bf16[256,4096]{1,0:T(8,128)(2,1)S(1)}, bf16[256,4096]{1,0:T(8,128)(2,1)}, u32[]{:S(2)}) copy-start(bf16[256,4096]{1,0:T(8,128)(2,1)} %y_hbm.1) | copy-start | bytes 6291460
  6.4 69.1 %all-to-all-start = ((bf16[64,272,128]{2,1,0:T(8,128)(2,1)}), bf16[64,272,128]{2,1,0:T(8,128)(2,1)}, u32[]{:S(2)}, u32[]{:S(2)}) async-start(bf16[64,272,128]{2,1,0:T(8,128)(2,1)} %send.1), calls=%async_computation | async-start | bytes 8912896 | tf_op jit(solution)/shard_map/all_to_all | solution.py:322

commit v5 on v4

--- a/solution.py
+++ b/solution.py
@@ -26,8 +26,8 @@
 
 
 def send_kernel(
-    dev_ref, slot_ref, x_ref, y_hbm, w_ref, out_ref, y_ref, probs, high_v, term, tail, edge_v, pos_v,
-    pos_s, sem, tail_sem, y_sem, pos_sem,
+    dev_ref, slot_ref, x_hbm, y_hbm, w_hbm, out_ref, yt_hbm, x_ref, w_ref, y_ref, yt_ref, probs, high_v, term, tail, edge_v, pos_v,
+    pos_s, sem, tail_sem, y_sem, yt_sem, pos_sem, x_sem, w_sem,
 ):
     rows, width = x_ref.shape
     owners = out_ref.shape[0]
@@ -38,8 +38,16 @@
     block_rows = halves * BLK
     padded = pos_v.shape[0]
 
+    def x_copy(h):
+        lanes = pl.ds(h * LANES, LANES)
+        return pltpu.make_async_copy(x_hbm.at[lanes], x_ref.at[lanes], x_sem.at[h])
+
+    for h in range(halves):
+        x_copy(h).start()
     y_copy = pltpu.make_async_copy(y_hbm, y_ref, y_sem)
     y_copy.start()
+    w_copy = pltpu.make_async_copy(w_hbm, w_ref, w_sem)
+    w_copy.start()
 
     edge_v[...] = jnp.full((8, LANES), -1.0, F32)
     edge_v[:topk, :blocks] = dev_ref[...].astype(F32)
@@ -75,6 +83,8 @@
             m = jnp.maximum(m, ref[lanes, t * LANES : (t + 1) * LANES])
         return jnp.max(m.astype(F32), axis=1, keepdims=True)
 
+    for h in range(halves):
+        x_copy(h).wait()
     teacher_high, teacher_sum = [], []
     for h in range(halves):
         lanes = slice(h * LANES, (h + 1) * LANES)
@@ -89,6 +99,7 @@
         teacher_sum.append(jnp.sum(total, axis=1, keepdims=True))
 
     y_copy.wait()
+    w_copy.wait()
     student_high = [shard_max(y_ref, h, student_tiles) for h in range(halves)]
 
     pos_copy.wait()
@@ -109,6 +120,13 @@
     mass = jnp.zeros((8, rows), F32)
     student_total = [jnp.zeros((LANES, LANES), F32) for _ in range(halves)]
     items = [(h, t) for h in range(halves) for t in range(student_tiles)]
+    yt_parts = yt_sem.shape[1]
+    yt_rows = student_tiles * LANES // yt_parts
+
+    def yt_copy(h, i):
+        part = pl.ds(i * yt_rows, yt_rows)
+        return pltpu.make_async_copy(yt_ref.at[h, part], yt_hbm.at[h, part], yt_sem.at[h, i])
+
     for q in range(pairs):
         w = w_ref[q * LANES : (q + 1) * LANES, :].astype(F32).T
         a0, a1 = w[:BLK], w[BLK:]
@@ -129,6 +147,11 @@
         for h, t in items[len(items) * q // pairs : len(items) * (q + 1) // pairs]:
             y = y_ref[h * LANES : (h + 1) * LANES, t * LANES : (t + 1) * LANES].astype(F32)
             student_total[h] = student_total[h] + jnp.exp2((y - high_v[h]) * EXP2_SCALE)
+            yt_ref[h, t * LANES : (t + 1) * LANES, :] = y_ref[
+                h * LANES : (h + 1) * LANES, t * LANES : (t + 1) * LANES
+            ].T
+            if (t + 1) * LANES % yt_rows == 0:
+                yt_copy(h, (t + 1) * LANES // yt_rows - 1).start()
         mass = mass + jnp.sum(u.reshape(4 * BLK // 8, 8, rows), axis=0)
         u = u.astype(BF16)
         for edge in range(2 * topk):
@@ -165,6 +188,9 @@
     tail_copy.start()
     pltpu.make_async_copy(term, term, sem).wait()
     tail_copy.wait()
+    for h in range(halves):
+        for i in range(yt_parts):
+            yt_copy(h, i).wait()
 
 
 def receive_kernel(
@@ -172,8 +198,7 @@
     bias, sem, tail_sem, code_sem, y_sem, out_sem,
 ):
     owners = arr_ref.shape[0]
-    width, rows = y_ref.shape
-    halves = rows // LANES
+    halves, width, _ = y_ref.shape
     tiles = width // LANES
     block_rows = halves * BLK
     groups = sem.shape[0]
@@ -258,7 +283,7 @@
         for h in range(halves):
             lanes = slice(h * LANES, (h + 1) * LANES)
             target = acc[pl.ds(pl.multiple_of(h * span + t * LANES, BLK), LANES), :]
-            goal = y_ref[cols, lanes].astype(F32) * EXP2_SCALE - bias[h : h + 1, :]
+            goal = y_ref[h, cols, :].astype(F32) * EXP2_SCALE - bias[h : h + 1, :]
             out_ref[lanes, cols] = (jnp.exp2(goal) - target).astype(BF16).T
             term = target * (jnp.log2(target) - goal)
             loss = loss + jnp.sum(term.reshape(LANES // 32, 32, LANES), axis=0)
@@ -298,13 +323,19 @@
     )
     vmem = pl.BlockSpec(memory_space=pltpu.VMEM)
     hbm = pl.BlockSpec(memory_space=pl.ANY)
-    outgoing = pl.pallas_call(
+    outgoing, learner_t = pl.pallas_call(
         send_kernel,
-        out_shape=jax.ShapeDtypeStruct((owners, packet_rows, LANES), BF16),
-        in_specs=[vmem, vmem, vmem, hbm, vmem],
-        out_specs=hbm,
+        out_shape=(
+            jax.ShapeDtypeStruct((owners, packet_rows, LANES), BF16),
+            jax.ShapeDtypeStruct((halves, width, LANES), BF16),
+        ),
+        in_specs=[vmem, vmem, hbm, hbm, hbm],
+        out_specs=(hbm, hbm),
         scratch_shapes=[
+            pltpu.VMEM((rows, teacher_width), BF16),
+            pltpu.VMEM(weight.shape, BF16),
             pltpu.VMEM((rows, width), BF16),
+            pltpu.VMEM((halves, width, LANES), BF16),
             pltpu.VMEM((teacher_width // LANES, rows, LANES), BF16),
             pltpu.VMEM((halves, LANES, LANES), F32),
             pltpu.VMEM((edges, block_rows, LANES), BF16),
@@ -315,6 +346,9 @@
             pltpu.SemaphoreType.DMA,
             pltpu.SemaphoreType.DMA,
             pltpu.SemaphoreType.DMA,
+            pltpu.SemaphoreType.DMA((halves, 4)),
+            pltpu.SemaphoreType.DMA,
+            pltpu.SemaphoreType.DMA((halves,)),
             pltpu.SemaphoreType.DMA,
         ],
         name="send",
@@ -329,7 +363,7 @@
         in_specs=[hbm, hbm],
         out_specs=(hbm, vmem),
         scratch_shapes=[
-            pltpu.VMEM((width, rows), BF16),
+            pltpu.VMEM((halves, width, LANES), BF16),
             pltpu.VMEM((rows, width), BF16),
             pltpu.VMEM((owners, MOST * block_rows, LANES), BF16),
             pltpu.VMEM((owners, TAIL_ROWS, LANES), BF16),
@@ -346,7 +380,7 @@
             pltpu.SemaphoreType.DMA((8,)),
         ],
         name="receive",
-    )(arrived, learner_score_matrix.T)
+    )(arrived, learner_t)
     parts = lax.all_to_all(loss, ("dp", "vocab"), split_axis=0, concat_axis=0, tiled=True)
     tokens = float(rows * lax.axis_size("dp"))
     unit = math.log(2.0) / (width * owners)

time: 101 us -> 98.9 us (0.979)
  blocking collectives: 15.7 us -> 82.4 us
  waiting for transfers between devices: 54.2 us -> 0 us
  starting transfers between devices: 12.3 us -> 0 us
  local copies, waits for them, and re-layouts: 2.58 us -> 0 us
    all_to_all x0 -> x1, blocking collectives: none -> 66.6 us  [per_device(): lax.all_to_all(outgoing, 'vocab', split_axis=0, concat_axis=0, tiled=True)]
    all_to_all x1 -> x0, waiting for transfers between devices: 54.2 us -> none  [per_device(): lax.all_to_all(outgoing, 'vocab', split_axis=0, concat_axis=0, tiled=True)]
    all_to_all x1 -> x0, starting transfers between devices: 12.3 us -> none  [per_device(): lax.all_to_all(outgoing, 'vocab', split_axis=0, concat_axis=0, tiled=True)]
    unnamed x3 -> x0, local copies, waits for them, and re-layouts: 2.58 us -> none
  transfers between devices with their start and end apart: 1 -> 0, of which waited for: 1 -> 0; matrix products, arithmetic and copies ran while one was open for 3% -> 0% of each run, Pallas kernels for 0% -> 0%
where the time goes in v5:
time: 98.9 us; the launch traced here: 98.7 us
  blocking collectives  82.4 us (83%)
  Pallas kernels  13 us (13%)
  between operations  2.43 us (2%)
    all_to_all x1, blocking collectives, per_device(): lax.all_to_all(outgoing, 'vocab', split_axis=0, concat_axis=0, tiled=True)  66.6 us
    all_to_all x1, blocking collectives, per_device(): lax.all_to_all(loss, ('dp', 'vocab'), split_axis=0, concat_axis=0, tiled=...  15.9 us
    pallas_call x1, Pallas kernels, per_device(): pl.pallas_call(receive_kernel, out_shape=(jax.ShapeDtypeStruct((rows, wid...  7.22 us
    pallas_call x1, Pallas kernels, per_device(): pl.pallas_call(send_kernel, out_shape=(jax.ShapeDtypeStruct((owners, pack...  5.83 us

profile of v5, /device:TPU:1, one launch (start us, length us, event | category | flops | bytes accessed | tf_op | source)
XLA Modules:
  0.0 98.7 jit_solution(14488579964209332954)
XLA Ops:
  0.6 5.8 %send.1 = (bf16[64,272,128]{2,1,0:T(8,128)(2,1)}, bf16[2,4096,128]{2,1,0:T(8,128)(2,1)}) custom-call(s32[2,30]{1,0:T(2,128)} %bitcast.8, s32[2,30]{1,0:T(2,128)} %bitcast.9, bf16[256,1920]{1,0:T(8,128)(2,1)} %x_hbm.1, bf16[256,4096]{1,0:T(8,128)(2,1)} %y_hbm.1, bf16[1920,128]{1,0:T(8,128)(2,1)} %bitcast.7), custom_call_target="tpu_custom_call" | custom-call | tf_op jit(solution)/shard_map/send/pallas_call | solution.py:326
  6.5 66.6 %all_to_all.10.arr_ref = bf16[64,272,128]{2,1,0:T(8,128)(2,1)} all-to-all(bf16[64,272,128]{2,1,0:T(8,128)(2,1)} %get-tuple-element.6), channel_id=1, replica_groups=mesh['dp'=2,'vocab'=64] {'vocab'}, dimensions={0} | all-to-all | bytes 8912896 | tf_op jit(solution)/shard_map/all_to_all | solution.py:356
  73.0 7.2 %receive.1 = (bf16[256,4096]{1,0:T(8,128)(2,1)}, f32[128,1,128]{2,1,0:T(1,128)}) custom-call(bf16[64,272,128]{2,1,0:T(8,128)(2,1)} %all_to_all.10.arr_ref, bf16[2,4096,128]{2,1,0:T(8,128)(2,1)} %get-tuple-element.7.y_hbm), custom_call_target="tpu_custom_call" | custom-call | tf_op jit(solution)/shard_map/receive/pallas_call | solution.py:357
  80.3 15.9 %all_to_all.11 = f32[128,1,128]{2,1,0:T(1,128)S(1)} all-to-all(f32[128,1,128]{2,1,0:T(1,128)} %get-tuple-element.9), channel_id=1, replica_groups=mesh['dp'=2,'vocab'=64] {'dp','vocab'}, dimensions={0} | all-to-all | bytes 131072 | tf_op jit(solution)/shard_map/all_to_all | solution.py:384
  96.1 0.7 reduce_sum.9

commit v6 on v5

--- a/solution.py
+++ b/solution.py
@@ -26,8 +26,8 @@
 
 
 def send_kernel(
-    dev_ref, slot_ref, x_hbm, y_hbm, w_hbm, out_ref, yt_hbm, x_ref, w_ref, y_ref, yt_ref, probs, high_v, term, tail, edge_v, pos_v,
-    pos_s, sem, tail_sem, y_sem, yt_sem, pos_sem, x_sem, w_sem,
+    dev_hbm, slot_hbm, x_hbm, y_hbm, w_hbm, out_ref, yt_ref, dev_ref, slot_ref, x_ref, w_ref, y_ref,
+    probs, high_v, edge_v, pos_v, pos_s, dev_sem, slot_sem, y_sem, pos_sem, x_sem, w_sem,
 ):
     rows, width = x_ref.shape
     owners = out_ref.shape[0]
@@ -42,6 +42,10 @@
         lanes = pl.ds(h * LANES, LANES)
         return pltpu.make_async_copy(x_hbm.at[lanes], x_ref.at[lanes], x_sem.at[h])
 
+    dev_copy = pltpu.make_async_copy(dev_hbm, dev_ref, dev_sem)
+    dev_copy.start()
+    slot_copy = pltpu.make_async_copy(slot_hbm, slot_ref, slot_sem)
+    slot_copy.start()
     for h in range(halves):
         x_copy(h).start()
     y_copy = pltpu.make_async_copy(y_hbm, y_ref, y_sem)
@@ -50,6 +54,8 @@
     w_copy.start()
 
     edge_v[...] = jnp.full((8, LANES), -1.0, F32)
+    dev_copy.wait()
+    slot_copy.wait()
     edge_v[:topk, :blocks] = dev_ref[...].astype(F32)
     edge_v[topk : 2 * topk, :blocks] = slot_ref[...].astype(F32)
     edge_rows = edge_v[...]
@@ -104,14 +110,6 @@
 
     pos_copy.wait()
 
-    def send_edges(q):
-        for index in range(q * 2 * topk, (q + 1) * 2 * topk):
-            place = pos_s[index // topk, index % topk]
-            at = pl.multiple_of((place % MOST) * block_rows, block_rows)
-            pltpu.make_async_copy(
-                term.at[index], out_ref.at[place // MOST, pl.ds(at, block_rows), :], sem
-            ).start()
-
     for h in range(halves):
         high_v[h] = jnp.broadcast_to(student_high[h], (LANES, LANES))
     lane = lax.broadcasted_iota(jnp.int32, (BLK, LANES), 1)
@@ -120,13 +118,6 @@
     mass = jnp.zeros((8, rows), F32)
     student_total = [jnp.zeros((LANES, LANES), F32) for _ in range(halves)]
     items = [(h, t) for h in range(halves) for t in range(student_tiles)]
-    yt_parts = yt_sem.shape[1]
-    yt_rows = student_tiles * LANES // yt_parts
-
-    def yt_copy(h, i):
-        part = pl.ds(i * yt_rows, yt_rows)
-        return pltpu.make_async_copy(yt_ref.at[h, part], yt_hbm.at[h, part], yt_sem.at[h, i])
-
     for q in range(pairs):
         w = w_ref[q * LANES : (q + 1) * LANES, :].astype(F32).T
         a0, a1 = w[:BLK], w[BLK:]
@@ -150,18 +141,15 @@
             yt_ref[h, t * LANES : (t + 1) * LANES, :] = y_ref[
                 h * LANES : (h + 1) * LANES, t * LANES : (t + 1) * LANES
             ].T
-            if (t + 1) * LANES % yt_rows == 0:
-                yt_copy(h, (t + 1) * LANES // yt_rows - 1).start()
         mass = mass + jnp.sum(u.reshape(4 * BLK // 8, 8, rows), axis=0)
         u = u.astype(BF16)
         for edge in range(2 * topk):
+            place = pos_s[2 * q + edge // topk, edge % topk]
+            at = pl.multiple_of((place % MOST) * block_rows, block_rows)
             for h in range(halves):
-                term[q * 2 * topk + edge, h * BLK : (h + 1) * BLK, :] = u[
+                out_ref[place // MOST, pl.ds(at + h * BLK, BLK), :] = u[
                     edge * BLK : (edge + 1) * BLK, h * LANES : (h + 1) * LANES
                 ]
-        if q > 0:
-            send_edges(q - 1)
-    send_edges(pairs - 1)
 
     row_lane = lax.broadcasted_iota(jnp.int32, (LANES, LANES), 1)
     r_hi, r_lo = split2(jnp.sum(mass, axis=0, keepdims=True))
@@ -181,57 +169,27 @@
         pieces.append(jnp.where(sub == CODE_ROW, codes, s))
     stats = jnp.concatenate(pieces, axis=0).astype(BF16)
     for i in range(owners):
-        tail[i] = stats
-    tail_copy = pltpu.make_async_copy(
-        tail, out_ref.at[:, pl.ds(MOST * block_rows, TAIL_ROWS), :], tail_sem
-    )
-    tail_copy.start()
-    pltpu.make_async_copy(term, term, sem).wait()
-    tail_copy.wait()
-    for h in range(halves):
-        for i in range(yt_parts):
-            yt_copy(h, i).wait()
+        out_ref[i, MOST * block_rows :, :] = stats
 
 
 def receive_kernel(
-    arr_ref, y_hbm, out_hbm, loss_ref, y_ref, out_ref, buf, tail, wide, scale, code_v, code_s, acc,
-    bias, sem, tail_sem, code_sem, y_sem, out_sem,
+    arr_ref, y_ref, out_hbm, loss_ref, out_ref, wide, scale, code_v, code_s, acc, bias, code_sem, out_sem
 ):
     owners = arr_ref.shape[0]
     halves, width, _ = y_ref.shape
     tiles = width // LANES
     block_rows = halves * BLK
-    groups = sem.shape[0]
-    per = owners // groups
     span = width + BLK
     vocab_width = float(width * owners)
     me = lax.axis_index("vocab")
 
-    tail_copy = pltpu.make_async_copy(
-        arr_ref.at[:, pl.ds(MOST * block_rows, TAIL_ROWS), :], tail, tail_sem
-    )
-    tail_copy.start()
-
-    def block_copy(g):
-        return pltpu.make_async_copy(
-            arr_ref.at[pl.ds(g * per, per), pl.ds(0, MOST * block_rows), :],
-            buf.at[pl.ds(g * per, per)],
-            sem.at[g],
-        )
-
-    for g in range(groups):
-        block_copy(g).start()
-    y_copy = pltpu.make_async_copy(y_hbm, y_ref, y_sem)
-    y_copy.start()
-
     for h in range(halves):
 
         @pl.loop(0, width // 512)
         def _(i):
             acc[pl.ds(pl.multiple_of(h * span + i * 512, BLK), 512), :] = jnp.full((512, LANES), TINY, F32)
 
-    tail_copy.wait()
-    wide[...] = tail[...].astype(F32).reshape(owners * TAIL_ROWS, LANES)
+    wide[...] = arr_ref[:, MOST * block_rows :, :].astype(F32).reshape(owners * TAIL_ROWS, LANES)
     codes = wide[pl.ds(CODE_ROW, owners, stride=TAIL_ROWS), :].astype(jnp.int32)
     code_v[...] = jnp.where(codes < 0, width // BLK, codes)
     code_copy = pltpu.make_async_copy(code_v, code_s, code_sem)
@@ -258,23 +216,19 @@
         row_terms = row_terms + total * (log_total - math.log2(vocab_width)) * (1.0 / owners)
 
     code_copy.wait()
-    for g in range(groups):
-        block_copy(g).wait()
-
-        def add_source(i, carry):
-            src = g * per + i
-            for slot in range(MOST):
-                c = code_s[src, me * MOST + slot]
-                for h in range(halves):
-                    at = pl.ds(pl.multiple_of(h * span + c * BLK, BLK), BLK)
-                    lo = slot * block_rows + h * BLK
-                    term = buf[src, lo : lo + BLK, :].astype(F32)
-                    acc[at, :] = acc[at, :] + term * scale[pl.ds(h * owners + src, 1), :]
-            return carry
-
-        lax.fori_loop(0, per, add_source, 0, unroll=2)
-
-    y_copy.wait()
+
+    def add_source(src, carry):
+        for slot in range(MOST):
+            c = code_s[src, me * MOST + slot]
+            for h in range(halves):
+                at = pl.ds(pl.multiple_of(h * span + c * BLK, BLK), BLK)
+                lo = slot * block_rows + h * BLK
+                term = arr_ref[src, lo : lo + BLK, :].astype(F32)
+                acc[at, :] = acc[at, :] + term * scale[pl.ds(h * owners + src, 1), :]
+        return carry
+
+    lax.fori_loop(0, owners, add_source, 0, unroll=4)
+
     chunks = out_sem.shape[0]
     chunk = width // chunks
 
@@ -311,7 +265,6 @@
     rows, teacher_width = mentor_score_matrix.shape
     width = learner_score_matrix.shape[1]
     tb_local, topk = align_dev.shape
-    edges = tb_local * topk
     halves = rows // LANES
     block_rows = halves * BLK
     packet_rows = MOST * block_rows + TAIL_ROWS
@@ -322,37 +275,40 @@
         .reshape(tb_local * chunks * topk, LANES)
     )
     vmem = pl.BlockSpec(memory_space=pltpu.VMEM)
-    hbm = pl.BlockSpec(memory_space=pl.ANY)
+    hbm = pl.BlockSpec(memory_space=pltpu.HBM)
+    params = pltpu.CompilerParams(vmem_limit_bytes=20 * 2**20)
     outgoing, learner_t = pl.pallas_call(
         send_kernel,
         out_shape=(
             jax.ShapeDtypeStruct((owners, packet_rows, LANES), BF16),
             jax.ShapeDtypeStruct((halves, width, LANES), BF16),
         ),
-        in_specs=[vmem, vmem, hbm, hbm, hbm],
-        out_specs=(hbm, hbm),
+        in_specs=[hbm] * 5,
+        out_specs=(vmem, vmem),
         scratch_shapes=[
+            pltpu.VMEM((topk, tb_local), jnp.int32),
+            pltpu.VMEM((topk, tb_local), jnp.int32),
             pltpu.VMEM((rows, teacher_width), BF16),
             pltpu.VMEM(weight.shape, BF16),
             pltpu.VMEM((rows, width), BF16),
-            pltpu.VMEM((halves, width, LANES), BF16),
             pltpu.VMEM((teacher_width // LANES, rows, LANES), BF16),
             pltpu.VMEM((halves, LANES, LANES), F32),
-            pltpu.VMEM((edges, block_rows, LANES), BF16),
-            pltpu.VMEM((owners, TAIL_ROWS, LANES), BF16),
             pltpu.VMEM((8, LANES), F32),
             pltpu.VMEM((32, LANES), jnp.int32),
             pltpu.SMEM((32, LANES), jnp.int32),
             pltpu.SemaphoreType.DMA,
             pltpu.SemaphoreType.DMA,
             pltpu.SemaphoreType.DMA,
-            pltpu.SemaphoreType.DMA((halves, 4)),
             pltpu.SemaphoreType.DMA,
             pltpu.SemaphoreType.DMA((halves,)),
             pltpu.SemaphoreType.DMA,
         ],
+        compiler_params=params,
         name="send",
-    )(align_dev.T, align_slot.T, mentor_score_matrix, learner_score_matrix, weight)
+    )(*(
+        pltpu.with_memory_space_constraint(a, pltpu.HBM)
+        for a in (align_dev.T, align_slot.T, mentor_score_matrix, learner_score_matrix, weight)
+    ))
     arrived = lax.all_to_all(outgoing, "vocab", split_axis=0, concat_axis=0, tiled=True)
     scaled_grad, loss = pl.pallas_call(
         receive_kernel,
@@ -360,25 +316,20 @@
             jax.ShapeDtypeStruct((rows, width), BF16),
             jax.ShapeDtypeStruct((shards, 1, LANES), F32),
         ),
-        in_specs=[hbm, hbm],
+        in_specs=[vmem, vmem],
         out_specs=(hbm, vmem),
         scratch_shapes=[
-            pltpu.VMEM((halves, width, LANES), BF16),
             pltpu.VMEM((rows, width), BF16),
-            pltpu.VMEM((owners, MOST * block_rows, LANES), BF16),
-            pltpu.VMEM((owners, TAIL_ROWS, LANES), BF16),
             pltpu.VMEM((owners * TAIL_ROWS, LANES), F32),
             pltpu.VMEM((halves * owners, LANES), F32),
             pltpu.VMEM((owners, LANES), jnp.int32),
             pltpu.SMEM((owners, LANES), jnp.int32),
             pltpu.VMEM((halves * (width + BLK), LANES), F32),
             pltpu.VMEM((8, LANES), F32),
-            pltpu.SemaphoreType.DMA((8,)),
-            pltpu.SemaphoreType.DMA,
-            pltpu.SemaphoreType.DMA,
             pltpu.SemaphoreType.DMA,
             pltpu.SemaphoreType.DMA((8,)),
         ],
+        compiler_params=params,
         name="receive",
     )(arrived, learner_t)
     parts = lax.all_to_all(loss, ("dp", "vocab"), split_axis=0, concat_axis=0, tiled=True)

time: 98.9 us -> 94.1 us (0.951)
  Pallas kernels: 13 us -> 8.82 us
    pallas_call x1, Pallas kernels: 7.22 us -> 4.79 us  [per_device(): pl.pallas_call(receive_kernel, out_shape=(jax.ShapeDtypeStruct((rows, wid...]
    pallas_call x1, Pallas kernels: 5.83 us -> 4.03 us  [per_device(): pl.pallas_call(send_kernel, out_shape=(jax.ShapeDtypeStruct((owners, pack...]
where the time goes in v6:
time: 94.1 us; the launch traced here: 93.9 us
  blocking collectives  82 us (87%)
  Pallas kernels  8.82 us (9%)
  between operations  2.43 us (3%)
    all_to_all x1, blocking collectives, per_device(): lax.all_to_all(outgoing, 'vocab', split_axis=0, concat_axis=0, tiled=True)  66.3 us
    all_to_all x1, blocking collectives, per_device(): lax.all_to_all(loss, ('dp', 'vocab'), split_axis=0, concat_axis=0, tiled=...  15.7 us
    pallas_call x1, Pallas kernels, per_device(): pl.pallas_call(receive_kernel, out_shape=(jax.ShapeDtypeStruct((rows, wid...  4.79 us
    pallas_call x1, Pallas kernels, per_device(): pl.pallas_call(send_kernel, out_shape=(jax.ShapeDtypeStruct((owners, pack...  4.03 us

profile of v6, /device:TPU:1, one launch (start us, length us, event | category | flops | bytes accessed | tf_op | source)
XLA Modules:
  0.0 93.9 jit_solution(4350958850387752087)
XLA Ops:
  0.6 4.0 %send.1 = (bf16[64,272,128]{2,1,0:T(8,128)(2,1)S(1)}, bf16[2,4096,128]{2,1,0:T(8,128)(2,1)S(1)}) custom-call(s32[2,30]{1,0:T(2,128)} %bitcast.8, s32[2,30]{1,0:T(2,128)} %bitcast.9, bf16[256,1920]{1,0:T(8,128)(2,1)} %x_hbm.1, bf16[256,4096]{1,0:T(8,128)(2,1)} %y_hbm.1, bf16[1920,128]{1,0:T(8,128)(2,1)} %bitcast.7), custom_call_target="tpu_custom_call" | custom-call | tf_op jit(solution)/shard_map/send/pallas_call | solution.py:280
  4.7 66.3 %all_to_all.10.arr_ref = bf16[64,272,128]{2,1,0:T(8,128)(2,1)S(1)} all-to-all(bf16[64,272,128]{2,1,0:T(8,128)(2,1)S(1)} %get-tuple-element.6), channel_id=1, replica_groups=mesh['dp'=2,'vocab'=64] {'vocab'}, dimensions={0} | all-to-all | bytes 8912896 | tf_op jit(solution)/shard_map/all_to_all | solution.py:312
  70.9 4.8 %receive.1 = (bf16[256,4096]{1,0:T(8,128)(2,1)}, f32[128,1,128]{2,1,0:T(1,128)S(1)}) custom-call(bf16[64,272,128]{2,1,0:T(8,128)(2,1)S(1)} %all_to_all.10.arr_ref, bf16[2,4096,128]{2,1,0:T(8,128)(2,1)S(1)} %get-tuple-element.7.y_ref), custom_call_target="tpu_custom_call" | custom-call | tf_op jit(solution)/shard_map/receive/pallas_call | solution.py:313
  75.7 15.7 %all_to_all.11 = f32[128,1,128]{2,1,0:T(1,128)S(1)} all-to-all(f32[128,1,128]{2,1,0:T(1,128)S(1)} %get-tuple-element.9), channel_id=1, replica_groups=mesh['dp'=2,'vocab'=64] {'dp','vocab'}, dimensions={0} | all-to-all | bytes 131072 | tf_op jit(solution)/shard_map/all_to_all | solution.py:335
  91.4 0.7 reduce_sum.9

commit v7 on v6

--- a/solution.py
+++ b/solution.py
@@ -26,7 +26,7 @@
 
 
 def send_kernel(
-    dev_hbm, slot_hbm, x_hbm, y_hbm, w_hbm, out_ref, yt_ref, dev_ref, slot_ref, x_ref, w_ref, y_ref,
+    dev_hbm, slot_hbm, x_hbm, y_hbm, w_hbm, out_ref, yt_ref, acc_ref, dev_ref, slot_ref, x_ref, w_ref, y_ref,
     probs, high_v, edge_v, pos_v, pos_s, dev_sem, slot_sem, y_sem, pos_sem, x_sem, w_sem,
 ):
     rows, width = x_ref.shape
@@ -89,6 +89,7 @@
             m = jnp.maximum(m, ref[lanes, t * LANES : (t + 1) * LANES])
         return jnp.max(m.astype(F32), axis=1, keepdims=True)
 
+    acc_ref[...] = jnp.full(acc_ref.shape, TINY, F32)
     for h in range(halves):
         x_copy(h).wait()
     teacher_high, teacher_sum = [], []
@@ -173,7 +174,8 @@
 
 
 def receive_kernel(
-    arr_ref, y_ref, out_hbm, loss_ref, out_ref, wide, scale, code_v, code_s, acc, bias, code_sem, out_sem
+    arr_ref, y_ref, acc_in, out_hbm, loss_ref, acc, out_ref, wide, scale, code_v, code_s, bias, code_sem,
+    out_sem,
 ):
     owners = arr_ref.shape[0]
     halves, width, _ = y_ref.shape
@@ -182,12 +184,6 @@
     span = width + BLK
     vocab_width = float(width * owners)
     me = lax.axis_index("vocab")
-
-    for h in range(halves):
-
-        @pl.loop(0, width // 512)
-        def _(i):
-            acc[pl.ds(pl.multiple_of(h * span + i * 512, BLK), 512), :] = jnp.full((512, LANES), TINY, F32)
 
     wide[...] = arr_ref[:, MOST * block_rows :, :].astype(F32).reshape(owners * TAIL_ROWS, LANES)
     codes = wide[pl.ds(CODE_ROW, owners, stride=TAIL_ROWS), :].astype(jnp.int32)
@@ -277,14 +273,16 @@
     vmem = pl.BlockSpec(memory_space=pltpu.VMEM)
     hbm = pl.BlockSpec(memory_space=pltpu.HBM)
     params = pltpu.CompilerParams(vmem_limit_bytes=20 * 2**20)
-    outgoing, learner_t = pl.pallas_call(
+    acc_shape = (halves * (width + BLK), LANES)
+    outgoing, learner_t, target = pl.pallas_call(
         send_kernel,
         out_shape=(
             jax.ShapeDtypeStruct((owners, packet_rows, LANES), BF16),
             jax.ShapeDtypeStruct((halves, width, LANES), BF16),
+            jax.ShapeDtypeStruct(acc_shape, F32),
         ),
         in_specs=[hbm] * 5,
-        out_specs=(vmem, vmem),
+        out_specs=(vmem, vmem, vmem),
         scratch_shapes=[
             pltpu.VMEM((topk, tb_local), jnp.int32),
             pltpu.VMEM((topk, tb_local), jnp.int32),
@@ -310,28 +308,29 @@
         for a in (align_dev.T, align_slot.T, mentor_score_matrix, learner_score_matrix, weight)
     ))
     arrived = lax.all_to_all(outgoing, "vocab", split_axis=0, concat_axis=0, tiled=True)
-    scaled_grad, loss = pl.pallas_call(
+    scaled_grad, loss, _ = pl.pallas_call(
         receive_kernel,
         out_shape=(
             jax.ShapeDtypeStruct((rows, width), BF16),
             jax.ShapeDtypeStruct((shards, 1, LANES), F32),
+            jax.ShapeDtypeStruct(acc_shape, F32),
         ),
-        in_specs=[vmem, vmem],
-        out_specs=(hbm, vmem),
+        in_specs=[vmem, vmem, vmem],
+        out_specs=(hbm, vmem, vmem),
+        input_output_aliases={2: 2},
         scratch_shapes=[
             pltpu.VMEM((rows, width), BF16),
             pltpu.VMEM((owners * TAIL_ROWS, LANES), F32),
             pltpu.VMEM((halves * owners, LANES), F32),
             pltpu.VMEM((owners, LANES), jnp.int32),
             pltpu.SMEM((owners, LANES), jnp.int32),
-            pltpu.VMEM((halves * (width + BLK), LANES), F32),
             pltpu.VMEM((8, LANES), F32),
             pltpu.SemaphoreType.DMA,
             pltpu.SemaphoreType.DMA((8,)),
         ],
         compiler_params=params,
         name="receive",
-    )(arrived, learner_t)
+    )(arrived, learner_t, target)
     parts = lax.all_to_all(loss, ("dp", "vocab"), split_axis=0, concat_axis=0, tiled=True)
     tokens = float(rows * lax.axis_size("dp"))
     unit = math.log(2.0) / (width * owners)

time: 94.1 us -> 93.8 us (level)
  no operation moved by 1% of the time
where the time goes in v7:
time: 93.8 us; the launch traced here: 93.6 us
  blocking collectives  81.9 us (87%)
  Pallas kernels  8.53 us (9%)
  between operations  2.43 us (3%)
    all_to_all x1, blocking collectives, per_device(): lax.all_to_all(outgoing, 'vocab', split_axis=0, concat_axis=0, tiled=True)  66.3 us
    all_to_all x1, blocking collectives, per_device(): lax.all_to_all(loss, ('dp', 'vocab'), split_axis=0, concat_axis=0, tiled=...  15.7 us
    pallas_call x1, Pallas kernels, per_device(): pl.pallas_call(receive_kernel, out_shape=(jax.ShapeDtypeStruct((rows, wid...  4.5 us
    pallas_call x1, Pallas kernels, per_device(): pl.pallas_call(send_kernel, out_shape=(jax.ShapeDtypeStruct((owners, pack...  4.03 us

profile of v7, /device:TPU:1, one launch (start us, length us, event | category | flops | bytes accessed | tf_op | source)
XLA Modules:
  0.0 93.6 jit_solution(14154591764004306116)
XLA Ops:
  0.6 4.0 %send.1 = (bf16[64,272,128]{2,1,0:T(8,128)(2,1)S(1)}, bf16[2,4096,128]{2,1,0:T(8,128)(2,1)S(1)}, f32[8320,128]{1,0:T(8,128)S(1)}) custom-call(s32[2,30]{1,0:T(2,128)} %bitcast.8, s32[2,30]{1,0:T(2,128)} %bitcast.9, bf16[256,1920]{1,0:T(8,128)(2,1)} %x_hbm.1, bf16[256,4096]{1,0:T(8,128)(2,1)} %y_hbm.1, bf16[1920,128]{1,0:T(8,128)(2,1)} %bitcast.7), custom_call_target="tpu_custom_call" | custom-call | tf_op jit(solution)/shard_map/send/pallas_call | solution.py:277
  4.7 66.3 %all_to_all.10.arr_ref = bf16[64,272,128]{2,1,0:T(8,128)(2,1)S(1)} all-to-all(bf16[64,272,128]{2,1,0:T(8,128)(2,1)S(1)} %get-tuple-element.7), channel_id=1, replica_groups=mesh['dp'=2,'vocab'=64] {'vocab'}, dimensions={0} | all-to-all | bytes 8912896 | tf_op jit(solution)/shard_map/all_to_all | solution.py:310
  70.9 4.5 %receive.1 = (bf16[256,4096]{1,0:T(8,128)(2,1)}, f32[128,1,128]{2,1,0:T(1,128)S(1)}, f32[8320,128]{1,0:T(8,128)S(1)}) custom-call(bf16[64,272,128]{2,1,0:T(8,128)(2,1)S(1)} %all_to_all.10.arr_ref, bf16[2,4096,128]{2,1,0:T(8,128)(2,1)S(1)} %get-tuple-element.8.y_ref, f32[8320,128]{1,0:T(8,128)S(1)} %get-tuple-element.9.acc_in), custom_call_target="tpu_custom_call", output_to_operand_aliasing={{2}: (2, {})} | custom-call | tf_op jit(solution)/shard_map/receive/pallas_call | solution.py:311
  75.4 15.7 %all_to_all.11 = f32[128,1,128]{2,1,0:T(1,128)S(1)} all-to-all(f32[128,1,128]{2,1,0:T(1,128)S(1)} %get-tuple-element.11), channel_id=1, replica_groups=mesh['dp'=2,'vocab'=64] {'dp','vocab'}, dimensions={0} | all-to-all | bytes 131072 | tf_op jit(solution)/shard_map/all_to_all | solution.py:334
  91.1 0.7 reduce_sum.9

commit v8 on v7

--- a/solution.py
+++ b/solution.py
@@ -1,3 +1,4 @@
+import functools
 import math
 
 import jax
@@ -26,7 +27,7 @@
 
 
 def send_kernel(
-    dev_hbm, slot_hbm, x_hbm, y_hbm, w_hbm, out_ref, yt_ref, acc_ref, dev_ref, slot_ref, x_ref, w_ref, y_ref,
+    dev_hbm, slot_hbm, x_hbm, y_hbm, w_hbm, out_ref, yt_ref, acc_lo, acc_hi, dev_ref, slot_ref, x_ref, w_ref, y_ref,
     probs, high_v, edge_v, pos_v, pos_s, dev_sem, slot_sem, y_sem, pos_sem, x_sem, w_sem,
 ):
     rows, width = x_ref.shape
@@ -89,7 +90,8 @@
             m = jnp.maximum(m, ref[lanes, t * LANES : (t + 1) * LANES])
         return jnp.max(m.astype(F32), axis=1, keepdims=True)
 
-    acc_ref[...] = jnp.full(acc_ref.shape, TINY, F32)
+    for acc in (acc_lo, acc_hi):
+        acc[...] = jnp.full(acc.shape, TINY, F32)
     for h in range(halves):
         x_copy(h).wait()
     teacher_high, teacher_sum = [], []
@@ -174,14 +176,14 @@
 
 
 def receive_kernel(
-    arr_ref, y_ref, acc_in, out_hbm, loss_ref, acc, out_ref, wide, scale, code_v, code_s, bias, code_sem,
-    out_sem,
+    arr_ref, y_ref, lo_in, hi_in, out_hbm, loss_ref, acc_lo, acc_hi, out_ref, wide, scale, code_v, code_s,
+    bias, code_sem, out_sem,
 ):
     owners = arr_ref.shape[0]
     halves, width, _ = y_ref.shape
     tiles = width // LANES
     block_rows = halves * BLK
-    span = width + BLK
+    accs = (acc_lo, acc_hi)
     vocab_width = float(width * owners)
     me = lax.axis_index("vocab")
 
@@ -217,7 +219,7 @@
         for slot in range(MOST):
             c = code_s[src, me * MOST + slot]
             for h in range(halves):
-                at = pl.ds(pl.multiple_of(h * span + c * BLK, BLK), BLK)
+                acc, at = accs[h], pl.ds(pl.multiple_of(c * BLK, BLK), BLK)
                 lo = slot * block_rows + h * BLK
                 term = arr_ref[src, lo : lo + BLK, :].astype(F32)
                 acc[at, :] = acc[at, :] + term * scale[pl.ds(h * owners + src, 1), :]
@@ -232,7 +234,7 @@
         cols = pl.ds(pl.multiple_of(t * LANES, LANES), LANES)
         for h in range(halves):
             lanes = slice(h * LANES, (h + 1) * LANES)
-            target = acc[pl.ds(pl.multiple_of(h * span + t * LANES, BLK), LANES), :]
+            target = accs[h][cols, :]
             goal = y_ref[h, cols, :].astype(F32) * EXP2_SCALE - bias[h : h + 1, :]
             out_ref[lanes, cols] = (jnp.exp2(goal) - target).astype(BF16).T
             term = target * (jnp.log2(target) - goal)
@@ -253,6 +255,10 @@
     )
     for copy in out_copies:
         copy.wait()
+
+
+def total_kernel(factor, parts_ref, out_ref):
+    out_ref[0] = jnp.sum(parts_ref[...]) * factor
 
 
 def per_device(mentor_score_matrix, learner_score_matrix, align_dev, align_slot, align_weight):
@@ -273,16 +279,17 @@
     vmem = pl.BlockSpec(memory_space=pltpu.VMEM)
     hbm = pl.BlockSpec(memory_space=pltpu.HBM)
     params = pltpu.CompilerParams(vmem_limit_bytes=20 * 2**20)
-    acc_shape = (halves * (width + BLK), LANES)
-    outgoing, learner_t, target = pl.pallas_call(
+    acc_shape = (width + BLK, LANES)
+    outgoing, learner_t, target_lo, target_hi = pl.pallas_call(
         send_kernel,
         out_shape=(
             jax.ShapeDtypeStruct((owners, packet_rows, LANES), BF16),
             jax.ShapeDtypeStruct((halves, width, LANES), BF16),
             jax.ShapeDtypeStruct(acc_shape, F32),
+            jax.ShapeDtypeStruct(acc_shape, F32),
         ),
         in_specs=[hbm] * 5,
-        out_specs=(vmem, vmem, vmem),
+        out_specs=(vmem, vmem, vmem, vmem),
         scratch_shapes=[
             pltpu.VMEM((topk, tb_local), jnp.int32),
             pltpu.VMEM((topk, tb_local), jnp.int32),
@@ -308,16 +315,17 @@
         for a in (align_dev.T, align_slot.T, mentor_score_matrix, learner_score_matrix, weight)
     ))
     arrived = lax.all_to_all(outgoing, "vocab", split_axis=0, concat_axis=0, tiled=True)
-    scaled_grad, loss, _ = pl.pallas_call(
+    scaled_grad, loss, _, _ = pl.pallas_call(
         receive_kernel,
         out_shape=(
             jax.ShapeDtypeStruct((rows, width), BF16),
             jax.ShapeDtypeStruct((shards, 1, LANES), F32),
             jax.ShapeDtypeStruct(acc_shape, F32),
+            jax.ShapeDtypeStruct(acc_shape, F32),
         ),
-        in_specs=[vmem, vmem, vmem],
-        out_specs=(hbm, vmem, vmem),
-        input_output_aliases={2: 2},
+        in_specs=[vmem, vmem, vmem, vmem],
+        out_specs=(hbm, vmem, vmem, vmem),
+        input_output_aliases={2: 2, 3: 3},
         scratch_shapes=[
             pltpu.VMEM((rows, width), BF16),
             pltpu.VMEM((owners * TAIL_ROWS, LANES), F32),
@@ -330,11 +338,18 @@
         ],
         compiler_params=params,
         name="receive",
-    )(arrived, learner_t, target)
+    )(arrived, learner_t, target_lo, target_hi)
     parts = lax.all_to_all(loss, ("dp", "vocab"), split_axis=0, concat_axis=0, tiled=True)
     tokens = float(rows * lax.axis_size("dp"))
     unit = math.log(2.0) / (width * owners)
-    divergence = SMOOTHING_HEAT * SMOOTHING_HEAT * unit / tokens * jnp.sum(parts)
+    divergence = pl.pallas_call(
+        functools.partial(total_kernel, SMOOTHING_HEAT * SMOOTHING_HEAT * unit / tokens),
+        out_shape=jax.ShapeDtypeStruct((1,), F32),
+        in_specs=[vmem],
+        out_specs=pl.BlockSpec(memory_space=pltpu.SMEM),
+        compiler_params=params,
+        name="total",
+    )(parts).reshape(())
     return scaled_grad, divergence
 
 

time: 93.8 us -> 92 us (0.981)
  between operations: 2.43 us -> 0.65 us
where the time goes in v8:
time: 92 us; the launch traced here: 91.8 us
  blocking collectives  82 us (89%)
  Pallas kernels  9.19 us (10%)
    all_to_all x1, blocking collectives, per_device(): lax.all_to_all(outgoing, 'vocab', split_axis=0, concat_axis=0, tiled=True)  66.3 us
    all_to_all x1, blocking collectives, per_device(): lax.all_to_all(loss, ('dp', 'vocab'), split_axis=0, concat_axis=0, tiled=...  15.7 us
    pallas_call x1, Pallas kernels, per_device(): pl.pallas_call(receive_kernel, out_shape=(jax.ShapeDtypeStruct((rows, wid...  4.4 us
    pallas_call x1, Pallas kernels, per_device(): pl.pallas_call(send_kernel, out_shape=(jax.ShapeDtypeStruct((owners, pack...  4.03 us

profile of v8, /device:TPU:1, one launch (start us, length us, event | category | flops | bytes accessed | tf_op | source)
XLA Modules:
  0.0 91.8 jit_solution(18385160667408544503)
XLA Ops:
  0.6 4.0 %send.1 = (bf16[64,272,128]{2,1,0:T(8,128)(2,1)S(1)}, bf16[2,4096,128]{2,1,0:T(8,128)(2,1)S(1)}, f32[4160,128]{1,0:T(8,128)S(1)}, f32[4160,128]{1,0:T(8,128)S(1)}) custom-call(s32[2,30]{1,0:T(2,128)} %bitcast.9, s32[2,30]{1,0:T(2,128)} %bitcast.10, bf16[256,1920]{1,0:T(8,128)(2,1)} %x_hbm.1, bf16[256,4096]{1,0:T(8,128)(2,1)} %y_hbm.1, bf16[1920,128]{1,0:T(8,128)(2,1)} %bitcast.8), custom_call_target="tpu_custom_call" | custom-call | tf_op jit(solution)/shard_map/send/pallas_call | solution.py:283
  4.7 66.3 %all_to_all.10.arr_ref = bf16[64,272,128]{2,1,0:T(8,128)(2,1)S(1)} all-to-all(bf16[64,272,128]{2,1,0:T(8,128)(2,1)S(1)} %get-tuple-element.8), channel_id=1, replica_groups=mesh['dp'=2,'vocab'=64] {'vocab'}, dimensions={0} | all-to-all | bytes 8912896 | tf_op jit(solution)/shard_map/all_to_all | solution.py:317
  70.9 4.4 %receive.1 = (bf16[256,4096]{1,0:T(8,128)(2,1)}, f32[128,1,128]{2,1,0:T(1,128)S(1)}, f32[4160,128]{1,0:T(8,128)S(1)}, f32[4160,128]{1,0:T(8,128)S(1)}) custom-call(bf16[64,272,128]{2,1,0:T(8,128)(2,1)S(1)} %all_to_all.10.arr_ref, bf16[2,4096,128]{2,1,0:T(8,128)(2,1)S(1)} %get-tuple-element.9.y_ref, ...), custom_call_target="tpu_custom_call", output_to_operand_aliasing={{2}: (2, {}), {3}: (3, {})} | custom-call | tf_op jit(solution)/shard_map/receive/pallas_call | solution.py:318
  75.3 15.7 %all_to_all.11.parts_ref = f32[128,1,128]{2,1,0:T(1,128)S(1)} all-to-all(f32[128,1,128]{2,1,0:T(1,128)S(1)} %get-tuple-element.13), channel_id=1, replica_groups=mesh['dp'=2,'vocab'=64] {'dp','vocab'}, dimensions={0} | all-to-all | bytes 131072 | tf_op jit(solution)/shard_map/all_to_all | solution.py:342
  91.1 0.8 total.1

commit v9 on v8

--- a/solution.py
+++ b/solution.py
@@ -135,6 +135,9 @@
             ],
             axis=0,
         ).astype(BF16)
+        both = jnp.sum((l0 + l1).reshape(BLK // 8, 8, LANES), axis=0)
+        both_hi, both_lo = split2(both)
+        lhs = jnp.concatenate([lhs, both_hi.astype(BF16), both_lo.astype(BF16)], axis=0)
         u = lax.dot_general(
             lhs, probs[q], (((1,), (1,)), ((), ())), preferred_element_type=F32
         )
@@ -144,8 +147,8 @@
             yt_ref[h, t * LANES : (t + 1) * LANES, :] = y_ref[
                 h * LANES : (h + 1) * LANES, t * LANES : (t + 1) * LANES
             ].T
-        mass = mass + jnp.sum(u.reshape(4 * BLK // 8, 8, rows), axis=0)
-        u = u.astype(BF16)
+        mass = mass + u[4 * BLK : 4 * BLK + 8] + u[4 * BLK + 8 :]
+        u = u[: 4 * BLK].astype(BF16)
         for edge in range(2 * topk):
             place = pos_s[2 * q + edge // topk, edge % topk]
             at = pl.multiple_of((place % MOST) * block_rows, block_rows)
@@ -225,7 +228,7 @@
                 acc[at, :] = acc[at, :] + term * scale[pl.ds(h * owners + src, 1), :]
         return carry
 
-    lax.fori_loop(0, owners, add_source, 0, unroll=4)
+    lax.fori_loop(0, owners, add_source, 0, unroll=8)
 
     chunks = out_sem.shape[0]
     chunk = width // chunks
@@ -334,7 +337,7 @@
             pltpu.SMEM((owners, LANES), jnp.int32),
             pltpu.VMEM((8, LANES), F32),
             pltpu.SemaphoreType.DMA,
-            pltpu.SemaphoreType.DMA((8,)),
+            pltpu.SemaphoreType.DMA((16,)),
         ],
         compiler_params=params,
         name="receive",

time: 92 us -> 92 us (level)
  no operation moved by 1% of the time
where the time goes in v9:
time: 92 us; the launch traced here: 91.8 us
  blocking collectives  82 us (89%)
  Pallas kernels  9.23 us (10%)
    all_to_all x1, blocking collectives, per_device(): lax.all_to_all(outgoing, 'vocab', split_axis=0, concat_axis=0, tiled=True)  66.3 us
    all_to_all x1, blocking collectives, per_device(): lax.all_to_all(loss, ('dp', 'vocab'), split_axis=0, concat_axis=0, tiled=...  15.7 us
    pallas_call x1, Pallas kernels, per_device(): pl.pallas_call(receive_kernel, out_shape=(jax.ShapeDtypeStruct((rows, wid...  4.42 us
    pallas_call x1, Pallas kernels, per_device(): pl.pallas_call(send_kernel, out_shape=(jax.ShapeDtypeStruct((owners, pack...  4.04 us

profile of v9, /device:TPU:1, one launch (start us, length us, event | category | flops | bytes accessed | tf_op | source)
XLA Modules:
  0.0 91.8 jit_solution(382930940834716301)
XLA Ops:
  0.6 4.0 %send.1 = (bf16[64,272,128]{2,1,0:T(8,128)(2,1)S(1)}, bf16[2,4096,128]{2,1,0:T(8,128)(2,1)S(1)}, f32[4160,128]{1,0:T(8,128)S(1)}, f32[4160,128]{1,0:T(8,128)S(1)}) custom-call(s32[2,30]{1,0:T(2,128)} %bitcast.9, s32[2,30]{1,0:T(2,128)} %bitcast.10, bf16[256,1920]{1,0:T(8,128)(2,1)} %x_hbm.1, bf16[256,4096]{1,0:T(8,128)(2,1)} %y_hbm.1, bf16[1920,128]{1,0:T(8,128)(2,1)} %bitcast.8), custom_call_target="tpu_custom_call" | custom-call | tf_op jit(solution)/shard_map/send/pallas_call | solution.py:286
  4.7 66.3 %all_to_all.10.arr_ref = bf16[64,272,128]{2,1,0:T(8,128)(2,1)S(1)} all-to-all(bf16[64,272,128]{2,1,0:T(8,128)(2,1)S(1)} %get-tuple-element.8), channel_id=1, replica_groups=mesh['dp'=2,'vocab'=64] {'vocab'}, dimensions={0} | all-to-all | bytes 8912896 | tf_op jit(solution)/shard_map/all_to_all | solution.py:320
  71.0 4.4 %receive.1 = (bf16[256,4096]{1,0:T(8,128)(2,1)}, f32[128,1,128]{2,1,0:T(1,128)S(1)}, f32[4160,128]{1,0:T(8,128)S(1)}, f32[4160,128]{1,0:T(8,128)S(1)}) custom-call(bf16[64,272,128]{2,1,0:T(8,128)(2,1)S(1)} %all_to_all.10.arr_ref, bf16[2,4096,128]{2,1,0:T(8,128)(2,1)S(1)} %get-tuple-element.9.y_ref, ...), custom_call_target="tpu_custom_call", output_to_operand_aliasing={{2}: (2, {}), {3}: (3, {})} | custom-call | tf_op jit(solution)/shard_map/receive/pallas_call | solution.py:321
  75.4 15.7 %all_to_all.11.parts_ref = f32[128,1,128]{2,1,0:T(1,128)S(1)} all-to-all(f32[128,1,128]{2,1,0:T(1,128)S(1)} %get-tuple-element.13), channel_id=1, replica_groups=mesh['dp'=2,'vocab'=64] {'dp','vocab'}, dimensions={0} | all-to-all | bytes 131072 | tf_op jit(solution)/shard_map/all_to_all | solution.py:345
  91.1 0.8 total.1
